TPU v7x, 32 devices: a whole 2x2x4 slice. The times are simulated.
32 devices in a mesh: batch: 8 (over z, x), owner: 4 (over y, core).
Axes of the slice: x: 2, y: 2, z: 4, core: 2. Of those that a mesh axis runs over, the one named last changes fastest.
Arguments:
- queries: bfloat16 [128, 32, 128], P(('batch', 'owner')), may hold values from -8 to 8
- pool: bfloat16 [32, 184, 128], P(('owner', 'batch')), may hold values from -20 to 20
- lengths: int32 [32], P('owner'), may hold values from 46 to 180, as said below
- candidates: int32 [128, 12], P('batch'), may hold values from 0 to 31, as said below
- owner_map: int32 [32], replicated, may hold values from 0 to 31, as said below
- teacher: float32 [128, 12], P(('batch', 'owner')), may hold values from -12 to 12
Outputs:
- query_grad: float32 [128, 32, 128], P(('batch', 'owner'))
- divergence: float32 [128], P(('batch', 'owner'))
Inputs may be any that keep to these rules, and one draw needn't show every extreme that they name: `lengths`: every owner group (pool rows k * 8 to (k + 1) * 8 - 1) holds a passage of exactly 180 tokens. `owner_map`: A permutation: each pool row belongs to one passage id. Each query names 12 different passages. The owner group of a passage p is owner_map[p] // 8. All queries of one batch index have the same number of candidates in each owner group: 6 in some of the groups, 3 in half, none in a quarter; which groups these are differs between batch indices.
All inputs are finite; a program needn't handle non-finite values.
Results may differ from a plain program's by a relative error of at most 0.0075.
Values may be sent and summed in bfloat16 or wider, within the bound.
No kernel may reach another device: no remote copies, remote signals or barrier semaphores. Data moves between devices by JAX's collectives and lax.ppermute only.
A program may use at most 64 MiB of HBM per device.

v0:
```python
import functools
import math

import jax
import jax.numpy as jnp
from jax import lax
from jax.experimental import pallas as pl
from jax.experimental.pallas import tpu as pltpu
from jax.sharding import PartitionSpec as P


SHARPNESS = 20.0
STUDENT_GAIN = 2.0
LOSS_SCALE = 64.0
EPSILON = 1e-06
LOG2E = math.log2(math.e)


VMEM_BUDGET = 24 << 20
STAGES = ((0,), (1,), (2,), (3, 4), (5,))
VMEM = pl.BlockSpec(memory_space=pltpu.VMEM)
SMEM = pl.BlockSpec(memory_space=pltpu.SMEM)


def norm_kernel(lengths_ref, pool_ref, out_ref):
    rows = pool_ref.shape[1]
    widened = pool_ref[0].astype(jnp.float32)
    inv = lax.rsqrt(jnp.sum(widened * widened, axis=-1, keepdims=True) + EPSILON)
    length = lengths_ref[lax.axis_index("batch")].astype(jnp.float32)
    last = lax.broadcasted_iota(jnp.int32, widened.shape, 0) == rows - 1
    out_ref[0] = jnp.where(last, length, widened * inv).astype(jnp.bfloat16)


def prep_kernel(order, cand_ref, map_ref, teacher_ref, query_ref,
                unit_ref, sent_ref, inv_ref, live_ref, target_ref, base_ref):
    own, toks, feat = query_ref.shape
    lanes = own * toks
    n_rows = len(order)
    qt = query_ref[...].reshape(lanes, feat).astype(jnp.float32).T
    inv = lax.rsqrt(jnp.sum(qt * qt, axis=0, keepdims=True) + EPSILON)
    unit = qt * inv
    unit_ref[...] = unit
    sent_ref[...] = unit.astype(jnp.bfloat16)
    inv_ref[...] = inv
    ncand = cand_ref.shape[1]
    group = lax.axis_index("owner")
    first = group * own
    me = group * lax.axis_size("batch") + lax.axis_index("batch")
    query_of = lax.broadcasted_iota(jnp.int32, (1, lanes), 1) // toks

    def spread(values):
        row = jnp.full((1, lanes), values[-1])
        for q in range(own - 1):
            row = jnp.where(query_of == q, values[q], row)
        return row

    teachers = [spread([teacher_ref[q, k] for q in range(own)]) for k in range(ncand)]
    log_total = jnp.log(sum(jnp.exp(t) for t in teachers))
    number = lax.broadcasted_iota(jnp.int32, (n_rows, lanes), 0)
    live = jnp.zeros((n_rows, lanes), jnp.float32)
    target = jnp.zeros((n_rows, lanes), jnp.float32)
    base = jnp.zeros((1, lanes), jnp.float32)
    mass = jnp.zeros((1, lanes), jnp.float32)
    for k in range(ncand):
        log_target = teachers[k] - log_total
        share = jnp.exp(log_target)
        base += share * log_target
        mass += share
        slot = spread([map_ref[cand_ref[first + q, k]] ^ me for q in range(own)])
        hit = number == slot
        live = jnp.where(hit, 1.0, live)
        target = jnp.where(hit, share, target)
    for place, delta in enumerate(order):
        live_ref[place:place + 1, :] = live[delta:delta + 1, :]
        target_ref[place:place + 1, :] = target[delta:delta + 1, :]
    base_ref[0:1, :] = base
    base_ref[1:2, :] = mass


def score_kernel(counts, start, toks, first, final, *refs):
    refs = list(refs)
    pieces = [refs.pop(0) for _ in counts]
    sent_ref, live_ref, target_ref = refs[:3]
    refs = refs[3:]
    if not first:
        told_ref, sums_in_ref = refs[:2]
        refs = refs[2:]
    if final:
        unit_ref, inv_ref, base_ref = refs[:3]
        refs = refs[3:]
        grad_ref, div_ref = refs[:2]
    else:
        told_out_ref, sums_ref = refs[:2]
    e_ref, tot_ref, cnt_ref = refs[2:]
    rows, lanes = e_ref.shape[1:]
    n = sum(counts)
    sent = sent_ref[...]
    token = lax.broadcasted_iota(jnp.int32, (rows, lanes), 0).astype(jnp.float32)
    where = [(ref, i) for ref, count in zip(pieces, counts) for i in range(count)]

    for j, (ref, i) in enumerate(where):
        block = ref[i]
        length = block[rows - 8:, :].astype(jnp.float32)[7:8, :]
        similar = jnp.dot(block, sent, preferred_element_type=jnp.float32)
        terms = jnp.where(token < length, jnp.exp2(similar * (SHARPNESS * LOG2E)), 0.0)
        e_ref[j] = terms
        tot_ref[j:j + 1, :] = jnp.sum(terms, axis=0, keepdims=True)
        cnt_ref[j:j + 1, :] = length

    totals = tot_ref[...]
    logs = jnp.log(totals / cnt_ref[...])
    same = (lax.broadcasted_iota(jnp.int32, (lanes, lanes), 0) // toks
            == lax.broadcasted_iota(jnp.int32, (lanes, lanes), 1) // toks).astype(jnp.float32)
    student = (STUDENT_GAIN / SHARPNESS) * jnp.dot(
        logs, same, precision=lax.Precision.HIGHEST, preferred_element_type=jnp.float32)
    target = target_ref[start:start + n, :]
    weight = live_ref[start:start + n, :] * jnp.exp(student)
    z = jnp.sum(weight, axis=0, keepdims=True)
    fit = jnp.sum(target * student, axis=0, keepdims=True)
    inverse = 1.0 / totals
    if first:
        told = jnp.zeros((2,) + sent.shape, jnp.float32)
        by_student, by_teacher = told[0], told[1]
    else:
        by_student, by_teacher = told_ref[0], told_ref[1]
        z += sums_in_ref[0:1, :]
        fit += sums_in_ref[1:2, :]

    for j, (ref, i) in enumerate(where):
        weights = (e_ref[j] * inverse[j:j + 1, :]).astype(jnp.bfloat16)
        mixed = lax.dot_general(ref[i], weights, (((0,), (0,)), ((), ())), preferred_element_type=jnp.float32)
        by_student += mixed * weight[j:j + 1, :]
        by_teacher += mixed * target[j:j + 1, :]

    if not final:
        told_out_ref[0] = by_student
        told_out_ref[1] = by_teacher
        sums_ref[0:1, :] = z
        sums_ref[1:2, :] = fit
        return
    unit_grad = (LOSS_SCALE * STUDENT_GAIN) * (by_student / z - by_teacher)
    unit = unit_ref[...]
    radial = jnp.sum(unit * unit_grad, axis=0, keepdims=True)
    out = (unit_grad - unit * radial) * inv_ref[...]
    grad_ref[...] = out.T
    div = base_ref[0:1, :] - fit + base_ref[1:2, :] * jnp.log(z)
    own = div_ref.shape[1]
    pick = (lax.broadcasted_iota(jnp.int32, (lanes, own), 0)
            == lax.broadcasted_iota(jnp.int32, (lanes, own), 1) * toks).astype(jnp.float32)
    div_ref[...] = jnp.dot(div, pick, precision=lax.Precision.HIGHEST, preferred_element_type=jnp.float32)


def exchange(value, axes, masks):
    sizes = [lax.axis_size(a) for a in axes]
    total = math.prod(sizes)

    def partner(i):
        out, rest = 0, i
        places = []
        for size in reversed(sizes):
            places.append(rest % size)
            rest //= size
        for place, size, mask in zip(reversed(places), sizes, masks):
            out = out * size + (place ^ mask)
        return out

    return lax.ppermute(value, axes if len(axes) > 1 else axes[0], [(i, partner(i)) for i in range(total)])


def gather_pool(block):
    nb, no = lax.axis_size("batch"), lax.axis_size("owner")
    far = [(("batch",), (1 << bit,), 1 << bit) for bit in range(1, nb.bit_length() - 1)]
    far += [(("owner",), (1 << bit,), nb << bit) for bit in range(2, no.bit_length() - 1)]
    near = [(("batch",), (1,), 1), (("owner",), (2,), 2 * nb), (("batch", "owner"), (1, 2), 2 * nb + 1)]

    def move(piece, step):
        axes, masks, delta = step
        return exchange(piece[0], axes, masks), [d ^ delta for d in piece[1]]

    def join(*pieces):
        return jnp.concatenate([v for v, _ in pieces], axis=0), [d for _, o in pieces for d in o]

    over = (("owner",), (1,), nb)
    held = (block, [0])
    for step in far[:-1]:
        held = join(held, move(held, step))
    rest = move(held, far[-1])
    beside = [move(held, step) for step in near]
    last = [move(rest, step) for step in near]
    mine = [held, rest]
    return [mine, beside, [move(join(*mine), over)], [move(join(*beside), over)], last, [move(join(*last), over)]]


def unit_rows(values):
    widened = values.astype(jnp.float32)
    inv_norm = lax.rsqrt(jnp.sum(widened * widened, axis=-1, keepdims=True) + EPSILON)
    return (widened * inv_norm, inv_norm)


def token_terms(query_block, passages, length_block):
    similar = jnp.einsum(
        "bid,bktd->bkit", query_block, passages, preferred_element_type=jnp.float32
    )
    in_range = lax.broadcasted_iota(jnp.int32, similar.shape, 3) < length_block[:, :, None, None]
    exp_terms = jnp.where(in_range, jnp.exp(SHARPNESS * similar), 0.0)
    return (exp_terms, jnp.sum(exp_terms, axis=3))


def loss_terms(scores, teacher_rows):
    student = STUDENT_GAIN * scores
    log_student = student - jnp.log(jnp.sum(jnp.exp(student), axis=1, keepdims=True))
    log_target = teacher_rows - jnp.log(jnp.sum(jnp.exp(teacher_rows), axis=1, keepdims=True))
    target = jnp.exp(log_target)
    divergence = jnp.sum(target * (log_target - log_student), axis=1)
    score_grad = LOSS_SCALE * STUDENT_GAIN * (jnp.exp(log_student) - target)
    return (divergence, score_grad)


def local_by_owner(queries, pool, lengths, candidates, owner_map, teacher):
    own_rows = queries.shape[0]
    all_rows = candidates.shape[0]
    tok_count = queries.shape[1]
    feature = queries.shape[2]
    slot_cap = 2 * (candidates.shape[1] // lax.axis_size("owner"))
    my_group = lax.axis_index("owner")
    unit_query, inv_norm = unit_rows(queries)
    sent_query = unit_query.astype(jnp.bfloat16)
    gathered = lax.all_gather(sent_query, "owner", axis=0, tiled=True)
    shard_unit = unit_rows(pool)[0].astype(jnp.bfloat16)
    cached = lax.all_gather(shard_unit, "batch", axis=0, tiled=True)
    group_rows = cached.shape[0]
    slot_ids = jnp.take(owner_map, candidates, axis=0)
    local_slot = slot_ids - my_group * group_rows
    is_local = (local_slot >= 0) & (local_slot < group_rows)
    order_rank = jnp.cumsum(is_local.astype(jnp.int32), axis=1) - 1
    slot_iota = lax.broadcasted_iota(jnp.int32, (1, 1, slot_cap), 2)
    matches = is_local[:, :, None] & (order_rank[:, :, None] == slot_iota)
    filled = jnp.any(matches, axis=1)
    pick_slot = jnp.sum(jnp.where(matches, local_slot[:, :, None], 0), axis=1)
    length_of = jnp.where(filled, jnp.take(lengths, pick_slot, axis=0), 1)

    def block_inputs(first_row, row_span):
        query_block = lax.dynamic_slice_in_dim(gathered, first_row, row_span, 0)
        pick_block = lax.dynamic_slice_in_dim(pick_slot, first_row, row_span, 0)
        length_block = lax.dynamic_slice_in_dim(length_of, first_row, row_span, 0)
        return (query_block, jnp.take(cached, pick_block, axis=0), length_block)

    stride = math.gcd(all_rows, 8)

    def forward(block_index):
        query_block, passages, length_block = block_inputs(block_index * stride, stride)
        totals = token_terms(query_block, passages, length_block)[1]
        ratio = totals / length_block[:, :, None].astype(jnp.float32)
        return jnp.sum(jnp.log(ratio), axis=2) / SHARPNESS

    slot_scores = lax.map(forward, jnp.arange(all_rows // stride)).reshape(all_rows, slot_cap)
    dense = jnp.sum(jnp.where(matches, slot_scores[:, None, :], 0.0), axis=2)
    own_scores = lax.psum_scatter(dense, "owner", scatter_dimension=0, tiled=True)
    divergence, grad_own = loss_terms(own_scores, teacher)
    grad_rows = lax.all_gather(grad_own, "owner", axis=0, tiled=True)
    slot_grads = jnp.sum(jnp.where(matches, grad_rows[:, :, None], 0.0), axis=1)
    groups = lax.axis_size("owner")
    inner = math.gcd(all_rows, 8)

    def one_block(block_index):
        first_row = 0 + block_index * inner
        query_block, passages, length_block = block_inputs(first_row, inner)
        grad_block = lax.dynamic_slice_in_dim(slot_grads, first_row, inner, 0)
        exp_terms, totals = token_terms(query_block, passages, length_block)
        weights = (exp_terms / totals[:, :, :, None]).astype(jnp.bfloat16)
        mixed = jnp.einsum("bkit,bktd->bkid", weights, passages, preferred_element_type=jnp.float32)
        return jnp.einsum("bk,bkid->bid", grad_block, mixed, precision=lax.Precision.HIGHEST)

    partials = (
        lax.map(one_block, jnp.arange(all_rows // inner))
        .reshape(all_rows, tok_count, feature)
        .reshape(groups, own_rows, tok_count, feature)
    )
    arrived = lax.all_to_all(partials, "owner", split_axis=0, concat_axis=0, tiled=True)
    unit_grad = jnp.sum(arrived, axis=0)
    radial = jnp.sum(unit_query * unit_grad, axis=-1, keepdims=True)
    query_grad = (unit_grad - unit_query * radial) * inv_norm
    return (query_grad, divergence)


def in_vmem(*values):
    return [pltpu.with_memory_space_constraint(v, pltpu.VMEM) for v in values]


def local_all(queries, pool, lengths, candidates, owner_map, teacher):
    own, toks, feat = queries.shape
    rows = pool.shape[1]
    lanes = own * toks
    f32 = jnp.float32
    block = pl.pallas_call(
        norm_kernel,
        out_shape=pltpu.VMEM(pool.shape, jnp.bfloat16),
        in_specs=[SMEM, VMEM],
        out_specs=VMEM,
        name="norm",
    )(lengths, pool)
    arrivals = gather_pool(block)
    stages = [sum((arrivals[i] for i in members), []) for members in STAGES]
    order = [d for stage in stages for _, offs in stage for d in offs]
    unit, sent, inv, live, target, base = pl.pallas_call(
        functools.partial(prep_kernel, order),
        out_shape=[
            pltpu.VMEM((feat, lanes), f32),
            pltpu.VMEM((feat, lanes), jnp.bfloat16),
            pltpu.VMEM((1, lanes), f32),
            pltpu.VMEM((len(order), lanes), f32),
            pltpu.VMEM((len(order), lanes), f32),
            pltpu.VMEM((2, lanes), f32),
        ],
        in_specs=[SMEM, SMEM, SMEM, VMEM],
        out_specs=[VMEM] * 6,
        name="prep",
    )(candidates, owner_map, teacher, queries)
    carry, start = (), 0
    for number, stage in enumerate(stages):
        counts = tuple(len(offs) for _, offs in stage)
        n = sum(counts)
        final = number == len(stages) - 1
        operands = [v for v, _ in stage] + [sent, live, target, *carry] + ([unit, inv, base] if final else [])
        if final:
            out_shape = [jax.ShapeDtypeStruct((lanes, feat), f32), jax.ShapeDtypeStruct((1, own), f32)]
        else:
            out_shape = [pltpu.VMEM((2, feat, lanes), f32), pltpu.VMEM((2, lanes), f32)]
        carry = pl.pallas_call(
            functools.partial(score_kernel, counts, start, toks, number == 0, final),
            out_shape=out_shape,
            in_specs=[VMEM] * len(operands),
            out_specs=[VMEM] * 2,
            scratch_shapes=[
                pltpu.VMEM((n, rows, lanes), f32),
                pltpu.VMEM((n, lanes), f32),
                pltpu.VMEM((n, lanes), f32),
            ],
        )(*in_vmem(*operands))
        start += n
    grad, div = carry
    return grad.reshape(own, toks, feat), div.reshape(own)


def local(queries, pool, lengths, candidates, owner_map, teacher):
    own, toks = queries.shape[:2]
    n_rows = lax.axis_size("batch") * lax.axis_size("owner")
    held = n_rows * pool.shape[1] * (4 * own * toks + 2 * pool.shape[2])
    plan = local_all if held <= VMEM_BUDGET else local_by_owner
    return plan(queries, pool, lengths, candidates, owner_map, teacher)


def solution(mesh):
    in_specs = (
        P(("batch", "owner"), None, None),
        P(("owner", "batch"), None, None),
        P("owner"),
        P("batch", None),
        P(),
        P(("batch", "owner"), None),
    )
    out_specs = (P(("batch", "owner"), None, None), P(("batch", "owner")))
    return jax.shard_map(local, mesh=mesh, in_specs=in_specs, out_specs=out_specs, check_vma=False)
```

profile of v0, /device:TPU:0, one launch (start us, length us, event | category | flops | bytes accessed | tf_op | source)
XLA Modules:
  0.0 27.4 jit_solution(13715608490634324342)
XLA Ops:
  0.6 0.9 %norm.1 = bf16[1,184,128]{2,1,0:T(8,128)(2,1)S(1)} custom-call(s32[8]{0:T(128)} %lengths_ref.1, bf16[1,184,128]{2,1,0:T(8,128)(2,1)} %pool_ref.1), custom_call_target="tpu_custom_call" | custom-call | tf_op jit(solution)/shard_map/norm/pallas_call | solution.py:295
  1.5 3.1 %collective-permute-start = (bf16[1,184,128]{2,1,0:T(8,128)(2,1)S(1)}, bf16[1,184,128]{2,1,0:T(8,128)(2,1)S(1)}, u32[]{:S(2)}, u32[]{:S(2)}) collective-permute-start(bf16[1,184,128]{2,1,0:T(8,128)(2,1)S(1)} %norm.1), channel_id=1, source_target_pairs={{0,8},{4,12},{8,0},{12,4},{16,24},{20,28},{24,16},{28,20},{1,9},{5... | collective-permute-start | bytes 141320 | tf_op jit(solution)/shard_map/ppermute | solution.py:167
  4.7 2.0 %collective-permute-done = bf16[1,184,128]{2,1,0:T(8,128)(2,1)S(1)} collective-permute-done((bf16[1,184,128]{2,1,0:T(8,128)(2,1)S(1)}, bf16[1,184,128]{2,1,0:T(8,128)(2,1)S(1)}, u32[]{:S(2)}, u32[]{:S(2)}) %collective-permute-start) | collective-permute-done | bytes 47136 | tf_op jit(solution)/shard_map/ppermute | solution.py:167
  6.7 3.1 %collective-permute-start.1 = (bf16[2,184,128]{2,1,0:T(8,128)(2,1)S(1)}, bf16[2,184,128]{2,1,0:T(8,128)(2,1)S(1)}, u32[]{:S(2)}, u32[]{:S(2)}) collective-permute-start(bf16[2,184,128]{2,1,0:T(8,128)(2,1)S(1)} %pad_maximum_fusion.3.refs_0_), channel_id=1, source_target_pairs={{0,16},{4,20},{8,24},{12,28},{16,0},{20,4},{24,8},{28,12},{1,17},{... | collective-permute-start | bytes 282632 | tf_op jit(solution)/shard_map/ppermute | solution.py:167
  9.8 1.5 %collective-permute-start.6 = (bf16[2,184,128]{2,1,0:T(8,128)(2,1)S(1)}, bf16[2,184,128]{2,1,0:T(8,128)(2,1)S(1)}, u32[]{:S(2)}, u32[]{:S(2)}) collective-permute-start(bf16[2,184,128]{2,1,0:T(8,128)(2,1)S(1)} %pad_maximum_fusion.3.refs_0_), channel_id=1, source_target_pairs={{0,4},{4,0},{8,12},{12,8},{16,20},{20,16},{24,28},{28,24},{1,5},{5... | collective-permute-start | bytes 282632 | tf_op jit(solution)/shard_map/ppermute | solution.py:167
  11.3 1.5 %collective-permute-start.7 = (bf16[2,184,128]{2,1,0:T(8,128)(2,1)S(1)}, bf16[2,184,128]{2,1,0:T(8,128)(2,1)S(1)}, u32[]{:S(2)}, u32[]{:S(2)}) collective-permute-start(bf16[2,184,128]{2,1,0:T(8,128)(2,1)S(1)} %pad_maximum_fusion.3.refs_0_), channel_id=1, source_target_pairs={{0,2},{1,3},{2,0},{3,1},{4,6},{5,7},{6,4},{7,5},{8,10},{9,11},{10,... | collective-permute-start | bytes 282632 | tf_op jit(solution)/shard_map/ppermute | solution.py:167
  12.8 0.5 %collective-permute-start.8 = (bf16[2,184,128]{2,1,0:T(8,128)(2,1)S(1)}, bf16[2,184,128]{2,1,0:T(8,128)(2,1)S(1)}, u32[]{:S(2)}, u32[]{:S(2)}) collective-permute-start(bf16[2,184,128]{2,1,0:T(8,128)(2,1)S(1)} %pad_maximum_fusion.3.refs_0_), channel_id=1, source_target_pairs={{0,6},{1,7},{2,4},{3,5},{4,2},{5,3},{6,0},{7,1},{8,14},{9,15},{10,... | collective-permute-start | bytes 282632 | tf_op jit(solution)/shard_map/ppermute | solution.py:167
  13.3 0.0 collective-permute-done.1.refs_1_
  13.3 1.5 %collective-permute-start.2 = (bf16[2,184,128]{2,1,0:T(8,128)(2,1)S(1)}, bf16[2,184,128]{2,1,0:T(8,128)(2,1)S(1)}, u32[]{:S(2)}, u32[]{:S(2)}) collective-permute-start(bf16[2,184,128]{2,1,0:T(8,128)(2,1)S(1)} %collective-permute-done.1.refs_1_), channel_id=1, source_target_pairs={{0,4},{4,0},{8,12},{12,8},{16,20},{20,16},{24,28},{28,24},{1,5},{5... | collective-permute-start | bytes 282632 | tf_op jit(solution)/shard_map/ppermute | solution.py:167
  14.8 1.5 %collective-permute-start.3 = (bf16[2,184,128]{2,1,0:T(8,128)(2,1)S(1)}, bf16[2,184,128]{2,1,0:T(8,128)(2,1)S(1)}, u32[]{:S(2)}, u32[]{:S(2)}) collective-permute-start(bf16[2,184,128]{2,1,0:T(8,128)(2,1)S(1)} %collective-permute-done.1.refs_1_), channel_id=1, source_target_pairs={{0,2},{1,3},{2,0},{3,1},{4,6},{5,7},{6,4},{7,5},{8,10},{9,11},{10,... | collective-permute-start | bytes 282632 | tf_op jit(solution)/shard_map/ppermute | solution.py:167
  16.3 0.0 collective-permute-done.6.refs_0_
  16.3 1.4 %collective-permute-start.4 = (bf16[2,184,128]{2,1,0:T(8,128)(2,1)S(1)}, bf16[2,184,128]{2,1,0:T(8,128)(2,1)S(1)}, u32[]{:S(2)}, u32[]{:S(2)}) collective-permute-start(bf16[2,184,128]{2,1,0:T(8,128)(2,1)S(1)} %collective-permute-done.1.refs_1_), channel_id=1, source_target_pairs={{0,6},{1,7},{2,4},{3,5},{4,2},{5,3},{6,0},{7,1},{8,14},{9,15},{10,... | collective-permute-start | bytes 282632 | tf_op jit(solution)/shard_map/ppermute | solution.py:167
  17.8 1.6 %collective-permute-done.7.refs_1_ = bf16[2,184,128]{2,1,0:T(8,128)(2,1)S(1)} collective-permute-done((bf16[2,184,128]{2,1,0:T(8,128)(2,1)S(1)}, bf16[2,184,128]{2,1,0:T(8,128)(2,1)S(1)}, u32[]{:S(2)}, u32[]{:S(2)}) %collective-permute-start.7) | collective-permute-done | bytes 94240 | tf_op jit(solution)/shard_map/ppermute | solution.py:167
  19.4 0.0 collective-permute-done.8.refs_2_
  19.4 0.1 collective-permute-start.9
  19.5 0.0 collective-permute-done.2.refs_1_
  19.5 0.9 %collective-permute-done.3.refs_2_ = bf16[2,184,128]{2,1,0:T(8,128)(2,1)S(1)} collective-permute-done((bf16[2,184,128]{2,1,0:T(8,128)(2,1)S(1)}, bf16[2,184,128]{2,1,0:T(8,128)(2,1)S(1)}, u32[]{:S(2)}, u32[]{:S(2)}) %collective-permute-start.3) | collective-permute-done | bytes 94240 | tf_op jit(solution)/shard_map/ppermute | solution.py:167
  20.4 1.4 %collective-permute-done.4.refs_3_ = bf16[2,184,128]{2,1,0:T(8,128)(2,1)S(1)} collective-permute-done((bf16[2,184,128]{2,1,0:T(8,128)(2,1)S(1)}, bf16[2,184,128]{2,1,0:T(8,128)(2,1)S(1)}, u32[]{:S(2)}, u32[]{:S(2)}) %collective-permute-start.4) | collective-permute-done | bytes 94240 | tf_op jit(solution)/shard_map/ppermute | solution.py:167
  21.8 0.1 collective-permute-start.5
  22.0 0.6 %collective-permute-start.10 = (bf16[4,184,128]{2,1,0:T(8,128)(2,1)S(1)}, bf16[4,184,128]{2,1,0:T(8,128)(2,1)S(1)}, u32[]{:S(2)}, u32[]{:S(2)}) collective-permute-start(bf16[4,184,128]{2,1,0:T(8,128)(2,1)S(1)} %pad_maximum_fusion.2), channel_id=1, source_target_pairs={{0,1},{1,0},{2,3},{3,2},{4,5},{5,4},{6,7},{7,6},{8,9},{9,8},{10,11... | collective-permute-start | bytes 565256 | tf_op jit(solution)/shard_map/ppermute | solution.py:167
  22.5 1.0 %prep.1 = (f32[128,128]{1,0:T(8,128)S(1)}, bf16[128,128]{1,0:T(8,128)(2,1)S(1)}, f32[1,128]{1,0:T(1,128)S(1)}, f32[32,128]{1,0:T(8,128)S(1)}, f32[32,128]{1,0:T(8,128)S(1)}, /*index=5*/f32[2,128]{1,0:T(2,128)S(1)}) custom-call(s32[16,12]{1,0:T(8,128)} %cand_ref.1, s32[32]{0:T(128)} %map_ref.1, f32[4,12]{1,0:T(4,128)} %teacher_ref.1, ...), custom_call_target="tpu_custom_call" | custom-call | tf_op jit(solution)/shard_map/prep/pallas_call | solution.py:305
  23.5 0.5 %shard_map.77 = (f32[2,128,128]{2,1,0:T(8,128)S(1)}, f32[2,128]{1,0:T(2,128)S(1)}) custom-call(bf16[2,184,128]{2,1,0:T(8,128)(2,1)S(1)} %pad_maximum_fusion.3.refs_0_, bf16[2,184,128]{2,1,0:T(8,128)(2,1)S(1)} %collective-permute-done.1.refs_1_, bf16[128,128]{1,0:T(8,128)(2,1)S(1)} %get-tuple-element.18.refs_2_.refs_3_.refs_1_.refs_4_, ...), custom_call_target="tpu_custom_call" | custom-call | tf_op jit(solution)/shard_map/pallas_call | solution.py:329
  24.0 0.6 %shard_map.78 = (f32[2,128,128]{2,1,0:T(8,128)S(1)}, f32[2,128]{1,0:T(2,128)S(1)}) custom-call(bf16[2,184,128]{2,1,0:T(8,128)(2,1)S(1)} %collective-permute-done.6.refs_0_, bf16[2,184,128]{2,1,0:T(8,128)(2,1)S(1)} %collective-permute-done.7.refs_1_, bf16[2,184,128]{2,1,0:T(8,128)(2,1)S(1)} %collective-permute-done.8.refs_2_, ...), custom_call_target="tpu_custom_call" | custom-call | tf_op jit(solution)/shard_map/pallas_call | solution.py:329
  24.6 0.0 collective-permute-done.10.refs_0_
  24.6 0.5 %shard_map.79 = (f32[2,128,128]{2,1,0:T(8,128)S(1)}, f32[2,128]{1,0:T(2,128)S(1)}) custom-call(bf16[4,184,128]{2,1,0:T(8,128)(2,1)S(1)} %collective-permute-done.10.refs_0_, bf16[128,128]{1,0:T(8,128)(2,1)S(1)} %get-tuple-element.18.refs_2_.refs_3_.refs_1_.refs_4_, f32[32,128]{1,0:T(8,128)S(1)} %get-tuple-element.19.refs_3_.refs_4_.refs_2_.refs_5_, ...), custom_call_target="tpu_custom_call" | custom-call | tf_op jit(solution)/shard_map/pallas_call | solution.py:329
  25.2 0.0 collective-permute-done.9.refs_0_
  25.2 0.8 %shard_map.80 = (f32[2,128,128]{2,1,0:T(8,128)S(1)}, f32[2,128]{1,0:T(2,128)S(1)}) custom-call(bf16[6,184,128]{2,1,0:T(8,128)(2,1)S(1)} %collective-permute-done.9.refs_0_, bf16[2,184,128]{2,1,0:T(8,128)(2,1)S(1)} %collective-permute-done.2.refs_1_, bf16[2,184,128]{2,1,0:T(8,128)(2,1)S(1)} %collective-permute-done.3.refs_2_, ...), custom_call_target="tpu_custom_call" | custom-call | tf_op jit(solution)/shard_map/pallas_call | solution.py:329
  26.0 0.0 collective-permute-done.5.refs_0_
  26.0 1.4 %shard_map.81 = (f32[128,128]{1,0:T(8,128)}, f32[1,4]{1,0:T(1,128)}) custom-call(bf16[6,184,128]{2,1,0:T(8,128)(2,1)S(1)} %collective-permute-done.5.refs_0_, bf16[128,128]{1,0:T(8,128)(2,1)S(1)} %get-tuple-element.18.refs_2_.refs_3_.refs_1_.refs_4_, f32[32,128]{1,0:T(8,128)S(1)} %get-tuple-element.19.refs_3_.refs_4_.refs_2_.refs_5_, ...), custom_call_target="tpu_custom_call" | custom-call | tf_op jit(solution)/shard_map/pallas_call | solution.py:329
  (4 shorter events, 0.1 us)
Async XLA Ops:
  1.5 5.2 %collective-permute-start = (bf16[1,184,128]{2,1,0:T(8,128)(2,1)S(1)}, bf16[1,184,128]{2,1,0:T(8,128)(2,1)S(1)}, u32[]{:S(2)}, u32[]{:S(2)}) collective-permute-start(bf16[1,184,128]{2,1,0:T(8,128)(2,1)S(1)} %norm.1), channel_id=1, source_target_pairs={{0,8},{4,12},{8,0},{12,4},{16,24},{20,28},{24,16},{28,20},{1,9},{5... | collective-permute-start | bytes 141320 | tf_op jit(solution)/shard_map/ppermute | solution.py:167
  6.7 6.6 %collective-permute-start.1 = (bf16[2,184,128]{2,1,0:T(8,128)(2,1)S(1)}, bf16[2,184,128]{2,1,0:T(8,128)(2,1)S(1)}, u32[]{:S(2)}, u32[]{:S(2)}) collective-permute-start(bf16[2,184,128]{2,1,0:T(8,128)(2,1)S(1)} %pad_maximum_fusion.3.refs_0_), channel_id=1, source_target_pairs={{0,16},{4,20},{8,24},{12,28},{16,0},{20,4},{24,8},{28,12},{1,17},{... | collective-permute-start | bytes 282632 | tf_op jit(solution)/shard_map/ppermute | solution.py:167
  9.8 6.5 %collective-permute-start.6 = (bf16[2,184,128]{2,1,0:T(8,128)(2,1)S(1)}, bf16[2,184,128]{2,1,0:T(8,128)(2,1)S(1)}, u32[]{:S(2)}, u32[]{:S(2)}) collective-permute-start(bf16[2,184,128]{2,1,0:T(8,128)(2,1)S(1)} %pad_maximum_fusion.3.refs_0_), channel_id=1, source_target_pairs={{0,4},{4,0},{8,12},{12,8},{16,20},{20,16},{24,28},{28,24},{1,5},{5... | collective-permute-start | bytes 282632 | tf_op jit(solution)/shard_map/ppermute | solution.py:167
  11.3 8.1 %collective-permute-start.7 = (bf16[2,184,128]{2,1,0:T(8,128)(2,1)S(1)}, bf16[2,184,128]{2,1,0:T(8,128)(2,1)S(1)}, u32[]{:S(2)}, u32[]{:S(2)}) collective-permute-start(bf16[2,184,128]{2,1,0:T(8,128)(2,1)S(1)} %pad_maximum_fusion.3.refs_0_), channel_id=1, source_target_pairs={{0,2},{1,3},{2,0},{3,1},{4,6},{5,7},{6,4},{7,5},{8,10},{9,11},{10,... | collective-permute-start | bytes 282632 | tf_op jit(solution)/shard_map/ppermute | solution.py:167
  12.8 6.6 %collective-permute-start.8 = (bf16[2,184,128]{2,1,0:T(8,128)(2,1)S(1)}, bf16[2,184,128]{2,1,0:T(8,128)(2,1)S(1)}, u32[]{:S(2)}, u32[]{:S(2)}) collective-permute-start(bf16[2,184,128]{2,1,0:T(8,128)(2,1)S(1)} %pad_maximum_fusion.3.refs_0_), channel_id=1, source_target_pairs={{0,6},{1,7},{2,4},{3,5},{4,2},{5,3},{6,0},{7,1},{8,14},{9,15},{10,... | collective-permute-start | bytes 282632 | tf_op jit(solution)/shard_map/ppermute | solution.py:167
  13.3 6.2 %collective-permute-start.2 = (bf16[2,184,128]{2,1,0:T(8,128)(2,1)S(1)}, bf16[2,184,128]{2,1,0:T(8,128)(2,1)S(1)}, u32[]{:S(2)}, u32[]{:S(2)}) collective-permute-start(bf16[2,184,128]{2,1,0:T(8,128)(2,1)S(1)} %collective-permute-done.1.refs_1_), channel_id=1, source_target_pairs={{0,4},{4,0},{8,12},{12,8},{16,20},{20,16},{24,28},{28,24},{1,5},{5... | collective-permute-start | bytes 282632 | tf_op jit(solution)/shard_map/ppermute | solution.py:167
  14.8 5.6 %collective-permute-start.3 = (bf16[2,184,128]{2,1,0:T(8,128)(2,1)S(1)}, bf16[2,184,128]{2,1,0:T(8,128)(2,1)S(1)}, u32[]{:S(2)}, u32[]{:S(2)}) collective-permute-start(bf16[2,184,128]{2,1,0:T(8,128)(2,1)S(1)} %collective-permute-done.1.refs_1_), channel_id=1, source_target_pairs={{0,2},{1,3},{2,0},{3,1},{4,6},{5,7},{6,4},{7,5},{8,10},{9,11},{10,... | collective-permute-start | bytes 282632 | tf_op jit(solution)/shard_map/ppermute | solution.py:167
  16.3 5.5 %collective-permute-start.4 = (bf16[2,184,128]{2,1,0:T(8,128)(2,1)S(1)}, bf16[2,184,128]{2,1,0:T(8,128)(2,1)S(1)}, u32[]{:S(2)}, u32[]{:S(2)}) collective-permute-start(bf16[2,184,128]{2,1,0:T(8,128)(2,1)S(1)} %collective-permute-done.1.refs_1_), channel_id=1, source_target_pairs={{0,6},{1,7},{2,4},{3,5},{4,2},{5,3},{6,0},{7,1},{8,14},{9,15},{10,... | collective-permute-start | bytes 282632 | tf_op jit(solution)/shard_map/ppermute | solution.py:167
  19.4 5.7 %collective-permute-start.9 = (bf16[6,184,128]{2,1,0:T(8,128)(2,1)S(1)}, bf16[6,184,128]{2,1,0:T(8,128)(2,1)S(1)}, u32[]{:S(2)}, u32[]{:S(2)}) collective-permute-start(bf16[6,184,128]{2,1,0:T(8,128)(2,1)S(1)} %pad_maximum_fusion.1), channel_id=1, source_target_pairs={{0,1},{1,0},{2,3},{3,2},{4,5},{5,4},{6,7},{7,6},{8,9},{9,8},{10,11... | collective-permute-start | bytes 847880 | tf_op jit(solution)/shard_map/ppermute | solution.py:167
  21.8 4.1 %collective-permute-start.5 = (bf16[6,184,128]{2,1,0:T(8,128)(2,1)S(1)}, bf16[6,184,128]{2,1,0:T(8,128)(2,1)S(1)}, u32[]{:S(2)}, u32[]{:S(2)}) collective-permute-start(bf16[6,184,128]{2,1,0:T(8,128)(2,1)S(1)} %pad_maximum_fusion), channel_id=1, source_target_pairs={{0,1},{1,0},{2,3},{3,2},{4,5},{5,4},{6,7},{7,6},{8,9},{9,8},{10,11... | collective-permute-start | bytes 847880 | tf_op jit(solution)/shard_map/ppermute | solution.py:167
  22.0 2.7 %collective-permute-start.10 = (bf16[4,184,128]{2,1,0:T(8,128)(2,1)S(1)}, bf16[4,184,128]{2,1,0:T(8,128)(2,1)S(1)}, u32[]{:S(2)}, u32[]{:S(2)}) collective-permute-start(bf16[4,184,128]{2,1,0:T(8,128)(2,1)S(1)} %pad_maximum_fusion.2), channel_id=1, source_target_pairs={{0,1},{1,0},{2,3},{3,2},{4,5},{5,4},{6,7},{7,6},{8,9},{9,8},{10,11... | collective-permute-start | bytes 565256 | tf_op jit(solution)/shard_map/ppermute | solution.py:167
where the time goes:
time: 27.6 us; the launch traced here: 27.4 us
  starting transfers between devices  14.8 us (54%)
  waiting for transfers between devices  5.98 us (22%)
  Pallas kernels  5.72 us (21%)
  between operations  0.74 us (3%)
    ppermute x11, starting transfers between devices, exchange(): lax.ppermute(value, axes if len(axes) > 1 else axes[0], [(i, partner(i))...  14.8 us
    ppermute x11, waiting for transfers between devices, exchange(): lax.ppermute(value, axes if len(axes) > 1 else axes[0], [(i, partner(i))...  5.98 us
    pallas_call x5, Pallas kernels, local_all(): pl.pallas_call(functools.partial(score_kernel, counts, start, toks, numbe...  3.85 us
    pallas_call x1, Pallas kernels, local_all(): pl.pallas_call(functools.partial(prep_kernel, order), out_shape=[pltpu.VM...  0.95 us
    pallas_call x1, Pallas kernels, local_all(): pl.pallas_call(norm_kernel, out_shape=pltpu.VMEM(pool.shape, jnp.bfloat16...  0.91 us
  transfers between devices with their start and end apart: 11, of which 4 were waited for; matrix products, arithmetic and copies ran while one was open for 0% of the time, Pallas kernels for 12%

commit v1 on v0

--- a/solution.py
+++ b/solution.py
@@ -17,7 +17,7 @@
 
 
 VMEM_BUDGET = 24 << 20
-STAGES = ((0,), (1,), (2,), (3, 4), (5,))
+STAGES = ((0,), (1,), (2,), (3, 4, 5), (6,))
 VMEM = pl.BlockSpec(memory_space=pltpu.VMEM)
 SMEM = pl.BlockSpec(memory_space=pltpu.SMEM)
 
@@ -36,45 +36,45 @@
     own, toks, feat = query_ref.shape
     lanes = own * toks
     n_rows = len(order)
-    qt = query_ref[...].reshape(lanes, feat).astype(jnp.float32).T
+    f32 = jnp.float32
+    qt = query_ref[...].reshape(lanes, feat).astype(f32).T
     inv = lax.rsqrt(jnp.sum(qt * qt, axis=0, keepdims=True) + EPSILON)
     unit = qt * inv
     unit_ref[...] = unit
     sent_ref[...] = unit.astype(jnp.bfloat16)
     inv_ref[...] = inv
-    ncand = cand_ref.shape[1]
     group = lax.axis_index("owner")
-    first = group * own
     me = group * lax.axis_size("batch") + lax.axis_index("batch")
-    query_of = lax.broadcasted_iota(jnp.int32, (1, lanes), 1) // toks
-
-    def spread(values):
-        row = jnp.full((1, lanes), values[-1])
-        for q in range(own - 1):
-            row = jnp.where(query_of == q, values[q], row)
-        return row
-
-    teachers = [spread([teacher_ref[q, k] for q in range(own)]) for k in range(ncand)]
-    log_total = jnp.log(sum(jnp.exp(t) for t in teachers))
-    number = lax.broadcasted_iota(jnp.int32, (n_rows, lanes), 0)
-    live = jnp.zeros((n_rows, lanes), jnp.float32)
-    target = jnp.zeros((n_rows, lanes), jnp.float32)
-    base = jnp.zeros((1, lanes), jnp.float32)
-    mass = jnp.zeros((1, lanes), jnp.float32)
-    for k in range(ncand):
-        log_target = teachers[k] - log_total
-        share = jnp.exp(log_target)
-        base += share * log_target
-        mass += share
-        slot = spread([map_ref[cand_ref[first + q, k]] ^ me for q in range(own)])
-        hit = number == slot
+
+    def by_lane(table, first):
+        row = lax.broadcasted_iota(jnp.int32, (table.shape[0], lanes), 0)
+        lane = lax.broadcasted_iota(jnp.int32, (table.shape[0], lanes), 1)
+        pick = (row == lane // toks + first).astype(f32)
+        return lax.dot_general(table, pick, (((0,), (0,)), ((), ())),
+                               precision=lax.Precision.HIGHEST, preferred_element_type=f32)
+
+    wanted = by_lane(cand_ref[...].astype(f32), group * own).astype(jnp.int32)
+    teachers = by_lane(teacher_ref[...], 0)
+    log_target = teachers - jnp.log(jnp.sum(jnp.exp(teachers), axis=0, keepdims=True))
+    share = jnp.exp(log_target)
+    base_ref[0:1, :] = jnp.sum(share * log_target, axis=0, keepdims=True)
+    base_ref[1:2, :] = jnp.sum(share, axis=0, keepdims=True)
+    passage = lax.broadcasted_iota(jnp.int32, (n_rows, lanes), 0)
+    live = jnp.zeros((n_rows, lanes), f32)
+    target = jnp.zeros((n_rows, lanes), f32)
+    for k in range(wanted.shape[0]):
+        hit = passage == wanted[k:k + 1, :]
         live = jnp.where(hit, 1.0, live)
-        target = jnp.where(hit, share, target)
-    for place, delta in enumerate(order):
-        live_ref[place:place + 1, :] = live[delta:delta + 1, :]
-        target_ref[place:place + 1, :] = target[delta:delta + 1, :]
-    base_ref[0:1, :] = base
-    base_ref[1:2, :] = mass
+        target = jnp.where(hit, share[k:k + 1, :], target)
+    place = lax.broadcasted_iota(jnp.int32, (n_rows, n_rows), 0)
+    delta = jnp.zeros((n_rows, n_rows), jnp.int32)
+    for number, value in enumerate(order):
+        delta = jnp.where(place == number, value, delta)
+    move = (map_ref[...] == (delta ^ me)).astype(f32)
+    both = jnp.dot(move, jnp.concatenate([live, target], axis=1),
+                   precision=lax.Precision.HIGHEST, preferred_element_type=f32)
+    live_ref[...] = both[:, :lanes]
+    target_ref[...] = both[:, lanes:]
 
 
 def score_kernel(counts, start, toks, first, final, *refs):
@@ -177,18 +177,32 @@
         axes, masks, delta = step
         return exchange(piece[0], axes, masks), [d ^ delta for d in piece[1]]
 
+    def both(one, two):
+        return one[0], (one[1][0] ^ two[1][0],), one[2] ^ two[2]
+
     def join(*pieces):
         return jnp.concatenate([v for v, _ in pieces], axis=0), [d for _, o in pieces for d in o]
 
     over = (("owner",), (1,), nb)
     held = (block, [0])
-    for step in far[:-1]:
-        held = join(held, move(held, step))
-    rest = move(held, far[-1])
+    low, high = (far + [None, None])[:2]
+    first = move(held, low)
+    second = move(held, high)
+    third = move(held, both(low, high))
+    held = join(held, first)
+    rest = join(second, third)
     beside = [move(held, step) for step in near]
     last = [move(rest, step) for step in near]
     mine = [held, rest]
-    return [mine, beside, [move(join(*mine), over)], [move(join(*beside), over)], last, [move(join(*last), over)]]
+    return [
+        mine,
+        beside,
+        [move(join(*mine), over)],
+        [move(join(*beside), over)],
+        last,
+        [move(join(*last[:2]), over)],
+        [move(last[2], over)],
+    ]
 
 
 def unit_rows(values):
@@ -312,10 +326,10 @@
             pltpu.VMEM((len(order), lanes), f32),
             pltpu.VMEM((2, lanes), f32),
         ],
-        in_specs=[SMEM, SMEM, SMEM, VMEM],
+        in_specs=[VMEM] * 4,
         out_specs=[VMEM] * 6,
         name="prep",
-    )(candidates, owner_map, teacher, queries)
+    )(*in_vmem(candidates, owner_map.reshape(1, -1), teacher, queries))
     carry, start = (), 0
     for number, stage in enumerate(stages):
         counts = tuple(len(offs) for _, offs in stage)

time: 27.6 us -> 29.9 us (1.083)
  waiting for transfers between devices: 5.98 us -> 9.62 us
  starting transfers between devices: 14.8 us -> 14.1 us
  Pallas kernels: 5.72 us -> 5.18 us
    ppermute x11 -> x13, waiting for transfers between devices: 5.98 us -> 9.62 us  [exchange(): lax.ppermute(value, axes if len(axes) > 1 else axes[0], [(i, partner(i))...]
    ppermute x11 -> x13, starting transfers between devices: 14.8 us -> 14.1 us  [exchange(): lax.ppermute(value, axes if len(axes) > 1 else axes[0], [(i, partner(i))...]
    pallas_call x1, Pallas kernels: 0.95 us -> 0.42 us  [local_all(): pl.pallas_call(functools.partial(prep_kernel, order), out_shape=[pltpu.VM...]
  transfers between devices with their start and end apart: 11 -> 13, of which waited for: 4 -> 5; matrix products, arithmetic and copies ran while one was open for 0% -> 0% of each run, Pallas kernels for 12% -> 10%
where the time goes in v1:
time: 29.9 us; the launch traced here: 29.8 us
  starting transfers between devices  14.1 us (47%)
  waiting for transfers between devices  9.62 us (32%)
  Pallas kernels  5.18 us (17%)
  between operations  0.8 us (3%)
    ppermute x13, starting transfers between devices, exchange(): lax.ppermute(value, axes if len(axes) > 1 else axes[0], [(i, partner(i))...  14.1 us
    ppermute x13, waiting for transfers between devices, exchange(): lax.ppermute(value, axes if len(axes) > 1 else axes[0], [(i, partner(i))...  9.62 us
    pallas_call x5, Pallas kernels, local_all(): pl.pallas_call(functools.partial(score_kernel, counts, start, toks, numbe...  3.84 us
    pallas_call x1, Pallas kernels, local_all(): pl.pallas_call(norm_kernel, out_shape=pltpu.VMEM(pool.shape, jnp.bfloat16...  0.91 us
  transfers between devices with their start and end apart: 13, of which 5 were waited for; matrix products, arithmetic and copies ran while one was open for 0% of the time, Pallas kernels for 10%

profile of v1, /device:TPU:0, one launch (start us, length us, event | category | flops | bytes accessed | tf_op | source)
XLA Modules:
  0.0 29.8 jit_solution(13478937895313581897)
XLA Ops:
  0.6 0.9 %norm.1 = bf16[1,184,128]{2,1,0:T(8,128)(2,1)S(1)} custom-call(s32[8]{0:T(128)} %lengths_ref.1, bf16[1,184,128]{2,1,0:T(8,128)(2,1)} %pool_ref.1), custom_call_target="tpu_custom_call" | custom-call | tf_op jit(solution)/shard_map/norm/pallas_call | solution.py:309
  1.5 3.1 %collective-permute-start.4 = (bf16[1,184,128]{2,1,0:T(8,128)(2,1)S(1)}, bf16[1,184,128]{2,1,0:T(8,128)(2,1)S(1)}, u32[]{:S(2)}, u32[]{:S(2)}) collective-permute-start(bf16[1,184,128]{2,1,0:T(8,128)(2,1)S(1)} %norm.1), channel_id=1, source_target_pairs={{0,8},{4,12},{8,0},{12,4},{16,24},{20,28},{24,16},{28,20},{1,9},{5... | collective-permute-start | bytes 141320 | tf_op jit(solution)/shard_map/ppermute | solution.py:167
  4.7 2.6 %collective-permute-start = (bf16[1,184,128]{2,1,0:T(8,128)(2,1)S(1)}, bf16[1,184,128]{2,1,0:T(8,128)(2,1)S(1)}, u32[]{:S(2)}, u32[]{:S(2)}) collective-permute-start(bf16[1,184,128]{2,1,0:T(8,128)(2,1)S(1)} %norm.1), channel_id=1, source_target_pairs={{0,16},{4,20},{8,24},{12,28},{16,0},{20,4},{24,8},{28,12},{1,17},{... | collective-permute-start | bytes 141320 | tf_op jit(solution)/shard_map/ppermute | solution.py:167
  7.3 0.0 collective-permute-start.1
  7.3 0.0 collective-permute-done.4
  7.3 1.8 %collective-permute-start.5 = (bf16[2,184,128]{2,1,0:T(8,128)(2,1)S(1)}, bf16[2,184,128]{2,1,0:T(8,128)(2,1)S(1)}, u32[]{:S(2)}, u32[]{:S(2)}) collective-permute-start(bf16[2,184,128]{2,1,0:T(8,128)(2,1)S(1)} %pad_maximum_fusion.3.refs_0_), channel_id=1, source_target_pairs={{0,4},{4,0},{8,12},{12,8},{16,20},{20,16},{24,28},{28,24},{1,5},{5... | collective-permute-start | bytes 282632 | tf_op jit(solution)/shard_map/ppermute | solution.py:167
  9.1 1.5 %collective-permute-start.6 = (bf16[2,184,128]{2,1,0:T(8,128)(2,1)S(1)}, bf16[2,184,128]{2,1,0:T(8,128)(2,1)S(1)}, u32[]{:S(2)}, u32[]{:S(2)}) collective-permute-start(bf16[2,184,128]{2,1,0:T(8,128)(2,1)S(1)} %pad_maximum_fusion.3.refs_0_), channel_id=1, source_target_pairs={{0,2},{1,3},{2,0},{3,1},{4,6},{5,7},{6,4},{7,5},{8,10},{9,11},{10,... | collective-permute-start | bytes 282632 | tf_op jit(solution)/shard_map/ppermute | solution.py:167
  10.6 0.3 collective-permute-start.7
  10.8 0.0 collective-permute-done
  10.8 2.3 %collective-permute-done.1 = bf16[1,184,128]{2,1,0:T(8,128)(2,1)S(1)} collective-permute-done((bf16[1,184,128]{2,1,0:T(8,128)(2,1)S(1)}, bf16[1,184,128]{2,1,0:T(8,128)(2,1)S(1)}, u32[]{:S(2)}, u32[]{:S(2)}) %collective-permute-start.1) | collective-permute-done | bytes 47136 | tf_op jit(solution)/shard_map/ppermute | solution.py:167
  13.1 1.6 %collective-permute-start.10 = (bf16[2,184,128]{2,1,0:T(8,128)(2,1)S(1)}, bf16[2,184,128]{2,1,0:T(8,128)(2,1)S(1)}, u32[]{:S(2)}, u32[]{:S(2)}) collective-permute-start(bf16[2,184,128]{2,1,0:T(8,128)(2,1)S(1)} %constant_dynamic-update-slice_fusion.refs_1_), channel_id=1, source_target_pairs={{0,2},{1,3},{2,0},{3,1},{4,6},{5,7},{6,4},{7,5},{8,10},{9,11},{10,... | collective-permute-start | bytes 282632 | tf_op jit(solution)/shard_map/ppermute | solution.py:167
  14.7 1.5 %collective-permute-start.9 = (bf16[2,184,128]{2,1,0:T(8,128)(2,1)S(1)}, bf16[2,184,128]{2,1,0:T(8,128)(2,1)S(1)}, u32[]{:S(2)}, u32[]{:S(2)}) collective-permute-start(bf16[2,184,128]{2,1,0:T(8,128)(2,1)S(1)} %constant_dynamic-update-slice_fusion.refs_1_), channel_id=1, source_target_pairs={{0,4},{4,0},{8,12},{12,8},{16,20},{20,16},{24,28},{28,24},{1,5},{5... | collective-permute-start | bytes 282632 | tf_op jit(solution)/shard_map/ppermute | solution.py:167
  16.2 0.1 collective-permute-start.12
  16.3 0.0 collective-permute-done.6.refs_1_
  16.3 0.5 %collective-permute-done.7.refs_2_ = bf16[2,184,128]{2,1,0:T(8,128)(2,1)S(1)} collective-permute-done((bf16[2,184,128]{2,1,0:T(8,128)(2,1)S(1)}, bf16[2,184,128]{2,1,0:T(8,128)(2,1)S(1)}, u32[]{:S(2)}, u32[]{:S(2)}) %collective-permute-start.7) | collective-permute-done | bytes 94240 | tf_op jit(solution)/shard_map/ppermute | solution.py:167
  16.9 0.0 copy-start
  16.9 0.0 copy-start.1
  16.9 0.1 collective-permute-start.8
  17.0 0.8 %collective-permute-done.10.refs_2_ = bf16[2,184,128]{2,1,0:T(8,128)(2,1)S(1)} collective-permute-done((bf16[2,184,128]{2,1,0:T(8,128)(2,1)S(1)}, bf16[2,184,128]{2,1,0:T(8,128)(2,1)S(1)}, u32[]{:S(2)}, u32[]{:S(2)}) %collective-permute-start.10) | collective-permute-done | bytes 94240 | tf_op jit(solution)/shard_map/ppermute | solution.py:167
  17.8 1.5 %collective-permute-done.9.refs_1_ = bf16[2,184,128]{2,1,0:T(8,128)(2,1)S(1)} collective-permute-done((bf16[2,184,128]{2,1,0:T(8,128)(2,1)S(1)}, bf16[2,184,128]{2,1,0:T(8,128)(2,1)S(1)}, u32[]{:S(2)}, u32[]{:S(2)}) %collective-permute-start.9) | collective-permute-done | bytes 94240 | tf_op jit(solution)/shard_map/ppermute | solution.py:167
  19.3 0.0 copy-start.3
  19.3 0.1 collective-permute-start.11
  19.4 1.5 %collective-permute-start.2 = (bf16[2,184,128]{2,1,0:T(8,128)(2,1)S(1)}, bf16[2,184,128]{2,1,0:T(8,128)(2,1)S(1)}, u32[]{:S(2)}, u32[]{:S(2)}) collective-permute-start(bf16[2,184,128]{2,1,0:T(8,128)(2,1)S(1)} %constant_dynamic-update-slice_fusion.refs_1_), channel_id=1, source_target_pairs={{0,6},{1,7},{2,4},{3,5},{4,2},{5,3},{6,0},{7,1},{8,14},{9,15},{10,... | collective-permute-start | bytes 282632 | tf_op jit(solution)/shard_map/ppermute | solution.py:167
  20.9 4.5 %collective-permute-done.2.refs_3_ = bf16[2,184,128]{2,1,0:T(8,128)(2,1)S(1)} collective-permute-done((bf16[2,184,128]{2,1,0:T(8,128)(2,1)S(1)}, bf16[2,184,128]{2,1,0:T(8,128)(2,1)S(1)}, u32[]{:S(2)}, u32[]{:S(2)}) %collective-permute-start.2) | collective-permute-done | bytes 94240 | tf_op jit(solution)/shard_map/ppermute | solution.py:167
  25.4 0.0 collective-permute-start.3
  25.4 0.4 %prep.1 = (f32[128,128]{1,0:T(8,128)S(1)}, bf16[128,128]{1,0:T(8,128)(2,1)S(1)}, f32[1,128]{1,0:T(1,128)S(1)}, f32[32,128]{1,0:T(8,128)S(1)}, f32[32,128]{1,0:T(8,128)S(1)}, /*index=5*/f32[2,128]{1,0:T(2,128)S(1)}) custom-call(s32[16,12]{1,0:T(8,128)S(1)} %copy-done.1, s32[1,32]{1,0:T(1,128)S(1)} %bitcast.3, f32[4,12]{1,0:T(4,128)S(1)} %copy-done.2, ...), custom_call_target="tpu_custom_call" | custom-call | tf_op jit(solution)/shard_map/prep/pallas_call | solution.py:319
  25.9 0.5 %shard_map.77 = (f32[2,128,128]{2,1,0:T(8,128)S(1)}, f32[2,128]{1,0:T(2,128)S(1)}) custom-call(bf16[2,184,128]{2,1,0:T(8,128)(2,1)S(1)} %pad_maximum_fusion.3.refs_0_, bf16[2,184,128]{2,1,0:T(8,128)(2,1)S(1)} %constant_dynamic-update-slice_fusion.refs_1_, bf16[128,128]{1,0:T(8,128)(2,1)S(1)} %get-tuple-element.18.refs_2_.refs_3_.refs_1_.refs_5_, ...), custom_call_target="tpu_custom_call" | custom-call | tf_op jit(solution)/shard_map/pallas_call | solution.py:343
  26.4 0.6 %shard_map.78 = (f32[2,128,128]{2,1,0:T(8,128)S(1)}, f32[2,128]{1,0:T(2,128)S(1)}) custom-call(bf16[2,184,128]{2,1,0:T(8,128)(2,1)S(1)} %collective-permute-done.5.refs_0_, bf16[2,184,128]{2,1,0:T(8,128)(2,1)S(1)} %collective-permute-done.6.refs_1_, bf16[2,184,128]{2,1,0:T(8,128)(2,1)S(1)} %collective-permute-done.7.refs_2_, ...), custom_call_target="tpu_custom_call" | custom-call | tf_op jit(solution)/shard_map/pallas_call | solution.py:343
  27.0 0.0 collective-permute-done.12.refs_0_
  27.0 0.5 %shard_map.79 = (f32[2,128,128]{2,1,0:T(8,128)S(1)}, f32[2,128]{1,0:T(2,128)S(1)}) custom-call(bf16[4,184,128]{2,1,0:T(8,128)(2,1)S(1)} %collective-permute-done.12.refs_0_, bf16[128,128]{1,0:T(8,128)(2,1)S(1)} %get-tuple-element.18.refs_2_.refs_3_.refs_1_.refs_5_, f32[32,128]{1,0:T(8,128)S(1)} %get-tuple-element.19.refs_3_.refs_4_.refs_2_.refs_6_, ...), custom_call_target="tpu_custom_call" | custom-call | tf_op jit(solution)/shard_map/pallas_call | solution.py:343
  27.6 1.0 %shard_map.80 = (f32[2,128,128]{2,1,0:T(8,128)S(1)}, f32[2,128]{1,0:T(2,128)S(1)}) custom-call(bf16[6,184,128]{2,1,0:T(8,128)(2,1)S(1)} %collective-permute-done.8.refs_0_, bf16[2,184,128]{2,1,0:T(8,128)(2,1)S(1)} %collective-permute-done.9.refs_1_, bf16[2,184,128]{2,1,0:T(8,128)(2,1)S(1)} %collective-permute-done.10.refs_2_, ...), custom_call_target="tpu_custom_call" | custom-call | tf_op jit(solution)/shard_map/pallas_call | solution.py:343
  28.6 1.2 %shard_map.81 = (f32[128,128]{1,0:T(8,128)}, f32[1,4]{1,0:T(1,128)}) custom-call(bf16[2,184,128]{2,1,0:T(8,128)(2,1)S(1)} %collective-permute-done.3.refs_0_, bf16[128,128]{1,0:T(8,128)(2,1)S(1)} %get-tuple-element.18.refs_2_.refs_3_.refs_1_.refs_5_, f32[32,128]{1,0:T(8,128)S(1)} %get-tuple-element.19.refs_3_.refs_4_.refs_2_.refs_6_, ...), custom_call_target="tpu_custom_call" | custom-call | tf_op jit(solution)/shard_map/pallas_call | solution.py:343
  (15 shorter events, 0.1 us)
Async XLA Ops:
  1.5 5.7 %collective-permute-start.4 = (bf16[1,184,128]{2,1,0:T(8,128)(2,1)S(1)}, bf16[1,184,128]{2,1,0:T(8,128)(2,1)S(1)}, u32[]{:S(2)}, u32[]{:S(2)}) collective-permute-start(bf16[1,184,128]{2,1,0:T(8,128)(2,1)S(1)} %norm.1), channel_id=1, source_target_pairs={{0,8},{4,12},{8,0},{12,4},{16,24},{20,28},{24,16},{28,20},{1,9},{5... | collective-permute-start | bytes 141320 | tf_op jit(solution)/shard_map/ppermute | solution.py:167
  4.7 6.2 %collective-permute-start = (bf16[1,184,128]{2,1,0:T(8,128)(2,1)S(1)}, bf16[1,184,128]{2,1,0:T(8,128)(2,1)S(1)}, u32[]{:S(2)}, u32[]{:S(2)}) collective-permute-start(bf16[1,184,128]{2,1,0:T(8,128)(2,1)S(1)} %norm.1), channel_id=1, source_target_pairs={{0,16},{4,20},{8,24},{12,28},{16,0},{20,4},{24,8},{28,12},{1,17},{... | collective-permute-start | bytes 141320 | tf_op jit(solution)/shard_map/ppermute | solution.py:167
  7.3 5.9 %collective-permute-start.1 = (bf16[1,184,128]{2,1,0:T(8,128)(2,1)S(1)}, bf16[1,184,128]{2,1,0:T(8,128)(2,1)S(1)}, u32[]{:S(2)}, u32[]{:S(2)}) collective-permute-start(bf16[1,184,128]{2,1,0:T(8,128)(2,1)S(1)} %norm.1), channel_id=1, source_target_pairs={{0,24},{4,28},{8,16},{12,20},{16,8},{20,12},{24,0},{28,4},{1,25},{... | collective-permute-start | bytes 141320 | tf_op jit(solution)/shard_map/ppermute | solution.py:167
  7.3 9.0 %collective-permute-start.5 = (bf16[2,184,128]{2,1,0:T(8,128)(2,1)S(1)}, bf16[2,184,128]{2,1,0:T(8,128)(2,1)S(1)}, u32[]{:S(2)}, u32[]{:S(2)}) collective-permute-start(bf16[2,184,128]{2,1,0:T(8,128)(2,1)S(1)} %pad_maximum_fusion.3.refs_0_), channel_id=1, source_target_pairs={{0,4},{4,0},{8,12},{12,8},{16,20},{20,16},{24,28},{28,24},{1,5},{5... | collective-permute-start | bytes 282632 | tf_op jit(solution)/shard_map/ppermute | solution.py:167
  9.1 7.3 %collective-permute-start.6 = (bf16[2,184,128]{2,1,0:T(8,128)(2,1)S(1)}, bf16[2,184,128]{2,1,0:T(8,128)(2,1)S(1)}, u32[]{:S(2)}, u32[]{:S(2)}) collective-permute-start(bf16[2,184,128]{2,1,0:T(8,128)(2,1)S(1)} %pad_maximum_fusion.3.refs_0_), channel_id=1, source_target_pairs={{0,2},{1,3},{2,0},{3,1},{4,6},{5,7},{6,4},{7,5},{8,10},{9,11},{10,... | collective-permute-start | bytes 282632 | tf_op jit(solution)/shard_map/ppermute | solution.py:167
  10.6 6.3 %collective-permute-start.7 = (bf16[2,184,128]{2,1,0:T(8,128)(2,1)S(1)}, bf16[2,184,128]{2,1,0:T(8,128)(2,1)S(1)}, u32[]{:S(2)}, u32[]{:S(2)}) collective-permute-start(bf16[2,184,128]{2,1,0:T(8,128)(2,1)S(1)} %pad_maximum_fusion.3.refs_0_), channel_id=1, source_target_pairs={{0,6},{1,7},{2,4},{3,5},{4,2},{5,3},{6,0},{7,1},{8,14},{9,15},{10,... | collective-permute-start | bytes 282632 | tf_op jit(solution)/shard_map/ppermute | solution.py:167
  13.1 4.7 %collective-permute-start.10 = (bf16[2,184,128]{2,1,0:T(8,128)(2,1)S(1)}, bf16[2,184,128]{2,1,0:T(8,128)(2,1)S(1)}, u32[]{:S(2)}, u32[]{:S(2)}) collective-permute-start(bf16[2,184,128]{2,1,0:T(8,128)(2,1)S(1)} %constant_dynamic-update-slice_fusion.refs_1_), channel_id=1, source_target_pairs={{0,2},{1,3},{2,0},{3,1},{4,6},{5,7},{6,4},{7,5},{8,10},{9,11},{10,... | collective-permute-start | bytes 282632 | tf_op jit(solution)/shard_map/ppermute | solution.py:167
  14.7 4.6 %collective-permute-start.9 = (bf16[2,184,128]{2,1,0:T(8,128)(2,1)S(1)}, bf16[2,184,128]{2,1,0:T(8,128)(2,1)S(1)}, u32[]{:S(2)}, u32[]{:S(2)}) collective-permute-start(bf16[2,184,128]{2,1,0:T(8,128)(2,1)S(1)} %constant_dynamic-update-slice_fusion.refs_1_), channel_id=1, source_target_pairs={{0,4},{4,0},{8,12},{12,8},{16,20},{20,16},{24,28},{28,24},{1,5},{5... | collective-permute-start | bytes 282632 | tf_op jit(solution)/shard_map/ppermute | solution.py:167
  16.2 10.8 %collective-permute-start.12 = (bf16[4,184,128]{2,1,0:T(8,128)(2,1)S(1)}, bf16[4,184,128]{2,1,0:T(8,128)(2,1)S(1)}, u32[]{:S(2)}, u32[]{:S(2)}) collective-permute-start(bf16[4,184,128]{2,1,0:T(8,128)(2,1)S(1)} %pad_maximum_fusion.2), channel_id=1, source_target_pairs={{0,1},{1,0},{2,3},{3,2},{4,5},{5,4},{6,7},{7,6},{8,9},{9,8},{10,11... | collective-permute-start | bytes 565256 | tf_op jit(solution)/shard_map/ppermute | solution.py:167
  16.9 8.5 %copy-start = (bf16[4,32,128]{2,1,0:T(8,128)(2,1)S(1)}, bf16[4,32,128]{2,1,0:T(8,128)(2,1)}, u32[]{:S(2)}) copy-start(bf16[4,32,128]{2,1,0:T(8,128)(2,1)} %query_ref.1) | copy-start | bytes 98308
  16.9 8.5 %copy-start.1 = (s32[16,12]{1,0:T(8,128)S(1)}, s32[16,12]{1,0:T(8,128)}, u32[]{:S(2)}) copy-start(s32[16,12]{1,0:T(8,128)} %cand_ref.1) | copy-start | bytes 2308
  16.9 10.6 %collective-permute-start.8 = (bf16[6,184,128]{2,1,0:T(8,128)(2,1)S(1)}, bf16[6,184,128]{2,1,0:T(8,128)(2,1)S(1)}, u32[]{:S(2)}, u32[]{:S(2)}) collective-permute-start(bf16[6,184,128]{2,1,0:T(8,128)(2,1)S(1)} %pad_maximum_fusion), channel_id=1, source_target_pairs={{0,1},{1,0},{2,3},{3,2},{4,5},{5,4},{6,7},{7,6},{8,9},{9,8},{10,11... | collective-permute-start | bytes 847880 | tf_op jit(solution)/shard_map/ppermute | solution.py:167
  19.3 6.1 %copy-start.2 = (f32[4,12]{1,0:T(4,128)S(1)}, f32[4,12]{1,0:T(4,128)}, u32[]{:S(2)}) copy-start(f32[4,12]{1,0:T(4,128)} %teacher_ref.1) | copy-start | bytes 580
  19.3 6.1 %copy-start.3 = (s32[32]{0:T(128)S(1)}, s32[32]{0:T(128)}, u32[]{:S(2)}) copy-start(s32[32]{0:T(128)} %param.10) | copy-start | bytes 388
  19.3 8.2 %collective-permute-start.11 = (bf16[4,184,128]{2,1,0:T(8,128)(2,1)S(1)}, bf16[4,184,128]{2,1,0:T(8,128)(2,1)S(1)}, u32[]{:S(2)}, u32[]{:S(2)}) collective-permute-start(bf16[4,184,128]{2,1,0:T(8,128)(2,1)S(1)} %pad_maximum_fusion.1), channel_id=1, source_target_pairs={{0,1},{1,0},{2,3},{3,2},{4,5},{5,4},{6,7},{7,6},{8,9},{9,8},{10,11... | collective-permute-start | bytes 565256 | tf_op jit(solution)/shard_map/ppermute | solution.py:167
  19.4 6.0 %collective-permute-start.2 = (bf16[2,184,128]{2,1,0:T(8,128)(2,1)S(1)}, bf16[2,184,128]{2,1,0:T(8,128)(2,1)S(1)}, u32[]{:S(2)}, u32[]{:S(2)}) collective-permute-start(bf16[2,184,128]{2,1,0:T(8,128)(2,1)S(1)} %constant_dynamic-update-slice_fusion.refs_1_), channel_id=1, source_target_pairs={{0,6},{1,7},{2,4},{3,5},{4,2},{5,3},{6,0},{7,1},{8,14},{9,15},{10,... | collective-permute-start | bytes 282632 | tf_op jit(solution)/shard_map/ppermute | solution.py:167
  25.4 3.1 %collective-permute-start.3 = (bf16[2,184,128]{2,1,0:T(8,128)(2,1)S(1)}, bf16[2,184,128]{2,1,0:T(8,128)(2,1)S(1)}, u32[]{:S(2)}, u32[]{:S(2)}) collective-permute-start(bf16[2,184,128]{2,1,0:T(8,128)(2,1)S(1)} %collective-permute-done.2.refs_3_), channel_id=1, source_target_pairs={{0,1},{1,0},{2,3},{3,2},{4,5},{5,4},{6,7},{7,6},{8,9},{9,8},{10,11... | collective-permute-start | bytes 282632 | tf_op jit(solution)/shard_map/ppermute | solution.py:167

commit v2 on v1

--- a/solution.py
+++ b/solution.py
@@ -17,25 +17,39 @@
 
 
 VMEM_BUDGET = 24 << 20
-STAGES = ((0,), (1,), (2,), (3, 4, 5), (6,))
+COST = 1 << 24
 VMEM = pl.BlockSpec(memory_space=pltpu.VMEM)
 SMEM = pl.BlockSpec(memory_space=pltpu.SMEM)
 
 
-def norm_kernel(lengths_ref, pool_ref, out_ref):
-    rows = pool_ref.shape[1]
-    widened = pool_ref[0].astype(jnp.float32)
-    inv = lax.rsqrt(jnp.sum(widened * widened, axis=-1, keepdims=True) + EPSILON)
-    length = lengths_ref[lax.axis_index("batch")].astype(jnp.float32)
-    last = lax.broadcasted_iota(jnp.int32, widened.shape, 0) == rows - 1
-    out_ref[0] = jnp.where(last, length, widened * inv).astype(jnp.bfloat16)
-
-
-def prep_kernel(order, cand_ref, map_ref, teacher_ref, query_ref,
+def norm_kernel(masks, lengths_ref, *refs):
+    out_ref = refs[-1]
+    rows = out_ref.shape[1]
+    lengths = lengths_ref[...].astype(jnp.float32)
+    place = lax.broadcasted_iota(jnp.int32, lengths.shape, 1)
+    last = lax.broadcasted_iota(jnp.int32, out_ref.shape[1:], 0) == rows - 1
+    for i, (mask, ref) in enumerate(zip(masks, refs)):
+        widened = ref[0].astype(jnp.float32)
+        inv = lax.rsqrt(jnp.sum(widened * widened, axis=-1, keepdims=True) + EPSILON)
+        theirs = place == lax.axis_index("batch") ^ mask
+        length = jnp.sum(jnp.where(theirs, lengths, 0.0), axis=1, keepdims=True)
+        out_ref[i] = jnp.where(last, length, widened * inv).astype(jnp.bfloat16)
+
+
+def order_kernel(order, out_ref):
+    me = lax.axis_index("owner") * lax.axis_size("batch") + lax.axis_index("batch")
+    place = lax.broadcasted_iota(jnp.int32, out_ref.shape, 0)
+    row = jnp.zeros(out_ref.shape, jnp.int32)
+    for number, delta in enumerate(order):
+        row = jnp.where(place == number, delta, row)
+    out_ref[...] = row ^ me
+
+
+def prep_kernel(order_ref, cand_ref, map_ref, teacher_ref, query_ref,
                 unit_ref, sent_ref, inv_ref, live_ref, target_ref, base_ref):
     own, toks, feat = query_ref.shape
     lanes = own * toks
-    n_rows = len(order)
+    n_rows = order_ref.shape[0]
     f32 = jnp.float32
     qt = query_ref[...].reshape(lanes, feat).astype(f32).T
     inv = lax.rsqrt(jnp.sum(qt * qt, axis=0, keepdims=True) + EPSILON)
@@ -44,7 +58,6 @@
     sent_ref[...] = unit.astype(jnp.bfloat16)
     inv_ref[...] = inv
     group = lax.axis_index("owner")
-    me = group * lax.axis_size("batch") + lax.axis_index("batch")
 
     def by_lane(table, first):
         row = lax.broadcasted_iota(jnp.int32, (table.shape[0], lanes), 0)
@@ -66,15 +79,20 @@
         hit = passage == wanted[k:k + 1, :]
         live = jnp.where(hit, 1.0, live)
         target = jnp.where(hit, share[k:k + 1, :], target)
-    place = lax.broadcasted_iota(jnp.int32, (n_rows, n_rows), 0)
-    delta = jnp.zeros((n_rows, n_rows), jnp.int32)
-    for number, value in enumerate(order):
-        delta = jnp.where(place == number, value, delta)
-    move = (map_ref[...] == (delta ^ me)).astype(f32)
+    move = (map_ref[...] == order_ref[...]).astype(f32)
     both = jnp.dot(move, jnp.concatenate([live, target], axis=1),
                    precision=lax.Precision.HIGHEST, preferred_element_type=f32)
     live_ref[...] = both[:, :lanes]
     target_ref[...] = both[:, lanes:]
+
+
+def exact_dot(values, picks):
+    parts = []
+    for _ in range(3):
+        parts.append(values.astype(jnp.bfloat16))
+        values = values - parts[-1].astype(jnp.float32)
+    return jnp.dot(jnp.concatenate(parts, axis=1), jnp.concatenate([picks] * 3, axis=0),
+                   preferred_element_type=jnp.float32)
 
 
 def score_kernel(counts, start, toks, first, final, *refs):
@@ -110,9 +128,8 @@
     totals = tot_ref[...]
     logs = jnp.log(totals / cnt_ref[...])
     same = (lax.broadcasted_iota(jnp.int32, (lanes, lanes), 0) // toks
-            == lax.broadcasted_iota(jnp.int32, (lanes, lanes), 1) // toks).astype(jnp.float32)
-    student = (STUDENT_GAIN / SHARPNESS) * jnp.dot(
-        logs, same, precision=lax.Precision.HIGHEST, preferred_element_type=jnp.float32)
+            == lax.broadcasted_iota(jnp.int32, (lanes, lanes), 1) // toks).astype(jnp.bfloat16)
+    student = (STUDENT_GAIN / SHARPNESS) * exact_dot(logs, same)
     target = target_ref[start:start + n, :]
     weight = live_ref[start:start + n, :] * jnp.exp(student)
     z = jnp.sum(weight, axis=0, keepdims=True)
@@ -138,7 +155,8 @@
         sums_ref[0:1, :] = z
         sums_ref[1:2, :] = fit
         return
-    unit_grad = (LOSS_SCALE * STUDENT_GAIN) * (by_student / z - by_teacher)
+    scale = LOSS_SCALE * STUDENT_GAIN
+    unit_grad = by_student * (scale / z) - scale * by_teacher
     unit = unit_ref[...]
     radial = jnp.sum(unit * unit_grad, axis=0, keepdims=True)
     out = (unit_grad - unit * radial) * inv_ref[...]
@@ -146,63 +164,33 @@
     div = base_ref[0:1, :] - fit + base_ref[1:2, :] * jnp.log(z)
     own = div_ref.shape[1]
     pick = (lax.broadcasted_iota(jnp.int32, (lanes, own), 0)
-            == lax.broadcasted_iota(jnp.int32, (lanes, own), 1) * toks).astype(jnp.float32)
-    div_ref[...] = jnp.dot(div, pick, precision=lax.Precision.HIGHEST, preferred_element_type=jnp.float32)
-
-
-def exchange(value, axes, masks):
-    sizes = [lax.axis_size(a) for a in axes]
-    total = math.prod(sizes)
-
-    def partner(i):
-        out, rest = 0, i
-        places = []
-        for size in reversed(sizes):
-            places.append(rest % size)
-            rest //= size
-        for place, size, mask in zip(reversed(places), sizes, masks):
-            out = out * size + (place ^ mask)
-        return out
-
-    return lax.ppermute(value, axes if len(axes) > 1 else axes[0], [(i, partner(i)) for i in range(total)])
-
-
-def gather_pool(block):
+            == lax.broadcasted_iota(jnp.int32, (lanes, own), 1) * toks).astype(jnp.bfloat16)
+    div_ref[...] = exact_dot(div, pick)
+
+
+def exchange(piece, db, do):
     nb, no = lax.axis_size("batch"), lax.axis_size("owner")
-    far = [(("batch",), (1 << bit,), 1 << bit) for bit in range(1, nb.bit_length() - 1)]
-    far += [(("owner",), (1 << bit,), nb << bit) for bit in range(2, no.bit_length() - 1)]
-    near = [(("batch",), (1,), 1), (("owner",), (2,), 2 * nb), (("batch", "owner"), (1, 2), 2 * nb + 1)]
-
-    def move(piece, step):
-        axes, masks, delta = step
-        return exchange(piece[0], axes, masks), [d ^ delta for d in piece[1]]
-
-    def both(one, two):
-        return one[0], (one[1][0] ^ two[1][0],), one[2] ^ two[2]
-
-    def join(*pieces):
-        return jnp.concatenate([v for v, _ in pieces], axis=0), [d for _, o in pieces for d in o]
-
-    over = (("owner",), (1,), nb)
-    held = (block, [0])
-    low, high = (far + [None, None])[:2]
-    first = move(held, low)
-    second = move(held, high)
-    third = move(held, both(low, high))
-    held = join(held, first)
-    rest = join(second, third)
-    beside = [move(held, step) for step in near]
-    last = [move(rest, step) for step in near]
+    pairs = [(b * no + o, (b ^ db) * no + (o ^ do)) for b in range(nb) for o in range(no)]
+    value = lax.ppermute(piece[0], ("batch", "owner"), pairs)
+    return value, [d ^ db ^ nb * do for d in piece[1]]
+
+
+def gather_pool(pool, normalize):
+    nb = lax.axis_size("batch")
+    masks = [2] + list(range(nb - 2, 2, -2))
+    raw = [exchange((pool, [0]), mask, 0)[0] for mask in masks]
+    held = normalize([0, masks[0]], [pool, raw[0]])
+    rest = normalize(masks[1:], raw[1:])
+    near = ((1, 0), (0, 2), (1, 2))
+    beside = [exchange(held, *way) for way in near]
+    last = [exchange(rest, *way) for way in near]
     mine = [held, rest]
-    return [
-        mine,
-        beside,
-        [move(join(*mine), over)],
-        [move(join(*beside), over)],
-        last,
-        [move(join(*last[:2]), over)],
-        [move(last[2], over)],
-    ]
+
+    def over(*pieces):
+        value = jnp.concatenate([v for v, _ in pieces], axis=0) if len(pieces) > 1 else pieces[0][0]
+        return exchange((value, [d for _, o in pieces for d in o]), 0, 1)
+
+    return [[*mine, *beside], [over(*mine)], [over(*beside), *last[:2]], [last[2], over(*last[:2])], [over(last[2])]]
 
 
 def unit_rows(values):
@@ -306,18 +294,28 @@
     rows = pool.shape[1]
     lanes = own * toks
     f32 = jnp.float32
-    block = pl.pallas_call(
-        norm_kernel,
-        out_shape=pltpu.VMEM(pool.shape, jnp.bfloat16),
-        in_specs=[SMEM, VMEM],
+
+    def normalize(masks, blocks):
+        value = pl.pallas_call(
+            functools.partial(norm_kernel, masks),
+            out_shape=pltpu.VMEM((len(masks), rows, feat), jnp.bfloat16),
+            in_specs=[VMEM] * (1 + len(masks)),
+            out_specs=VMEM,
+            name="norm",
+        )(*in_vmem(lengths.reshape(1, -1), *blocks))
+        return value, list(masks)
+
+    stages = gather_pool(pool, normalize)
+    order = [d for stage in stages for _, offs in stage for d in offs]
+    numbers = pl.pallas_call(
+        functools.partial(order_kernel, order),
+        out_shape=pltpu.VMEM((len(order), len(order)), jnp.int32),
         out_specs=VMEM,
-        name="norm",
-    )(lengths, pool)
-    arrivals = gather_pool(block)
-    stages = [sum((arrivals[i] for i in members), []) for members in STAGES]
-    order = [d for stage in stages for _, offs in stage for d in offs]
+        cost_estimate=pl.CostEstimate(flops=COST, bytes_accessed=COST, transcendentals=0),
+        name="order",
+    )()
     unit, sent, inv, live, target, base = pl.pallas_call(
-        functools.partial(prep_kernel, order),
+        prep_kernel,
         out_shape=[
             pltpu.VMEM((feat, lanes), f32),
             pltpu.VMEM((feat, lanes), jnp.bfloat16),
@@ -326,13 +324,13 @@
             pltpu.VMEM((len(order), lanes), f32),
             pltpu.VMEM((2, lanes), f32),
         ],
-        in_specs=[VMEM] * 4,
+        in_specs=[VMEM] * 5,
         out_specs=[VMEM] * 6,
         name="prep",
-    )(*in_vmem(candidates, owner_map.reshape(1, -1), teacher, queries))
+    )(*in_vmem(numbers, candidates, owner_map.reshape(1, -1), teacher, queries))
     carry, start = (), 0
     for number, stage in enumerate(stages):
-        counts = tuple(len(offs) for _, offs in stage)
+        counts = tuple(value.shape[0] for value, _ in stage)
         n = sum(counts)
         final = number == len(stages) - 1
         operands = [v for v, _ in stage] + [sent, live, target, *carry] + ([unit, inv, base] if final else [])
@@ -360,7 +358,9 @@
     own, toks = queries.shape[:2]
     n_rows = lax.axis_size("batch") * lax.axis_size("owner")
     held = n_rows * pool.shape[1] * (4 * own * toks + 2 * pool.shape[2])
-    plan = local_all if held <= VMEM_BUDGET else local_by_owner
+    nb = lax.axis_size("batch")
+    paired = nb >= 8 and nb & (nb - 1) == 0 and lax.axis_size("owner") == 4
+    plan = local_all if paired and held <= VMEM_BUDGET else local_by_owner
     return plan(queries, pool, lengths, candidates, owner_map, teacher)
 
 

time: 29.9 us -> 29.3 us (0.980)
  waiting for transfers between devices: 9.62 us -> 8.08 us
  local copies, waits for them, and re-layouts: 0.04 us -> 1.48 us
  Pallas kernels: 5.18 us -> 4.27 us
  starting transfers between devices: 14.1 us -> 14.4 us
    ppermute x13, waiting for transfers between devices: 9.62 us -> 8.08 us  [exchange(): value = lax.ppermute(piece[0], ('batch', 'owner'), pairs)]
    unnamed x9 -> x12, local copies, waits for them, and re-layouts: 0.03 us -> 1.48 us
    pallas_call x2 -> x4, Pallas kernels: 1.33 us -> 0.69 us  [the longest x1 0.42 us: local_all(): pl.pallas_call(prep_kernel, out_shape=[pltpu.VMEM((feat, lanes), f32), pl...]
    ppermute x13, starting transfers between devices: 14.1 us -> 14.4 us  [exchange(): value = lax.ppermute(piece[0], ('batch', 'owner'), pairs)]
  transfers between devices with their start and end apart: 13 -> 13, of which waited for: 5 -> 5; matrix products, arithmetic and copies ran while one was open for 0% -> 0% of each run, Pallas kernels for 10% -> 11%
where the time goes in v2:
time: 29.3 us; the launch traced here: 29.1 us
  starting transfers between devices  14.4 us (49%)
  waiting for transfers between devices  8.08 us (28%)
  Pallas kernels  4.27 us (15%)
  local copies, waits for them, and re-layouts  1.48 us (5%)
  between operations  0.8 us (3%)
    ppermute x13, starting transfers between devices, exchange(): value = lax.ppermute(piece[0], ('batch', 'owner'), pairs)  14.4 us
    ppermute x13, waiting for transfers between devices, exchange(): value = lax.ppermute(piece[0], ('batch', 'owner'), pairs)  8.08 us
    pallas_call x5, Pallas kernels, local_all(): pl.pallas_call(functools.partial(score_kernel, counts, start, toks, numbe...  3.58 us
    unnamed x12, local copies, waits for them, and re-layouts  1.48 us
  transfers between devices with their start and end apart: 13, of which 5 were waited for; matrix products, arithmetic and copies ran while one was open for 0% of the time, Pallas kernels for 11%

profile of v2, /device:TPU:0, one launch (start us, length us, event | category | flops | bytes accessed | tf_op | source)
XLA Modules:
  0.0 29.1 jit_solution(12931312073436028727)
XLA Ops:
  0.6 3.1 %collective-permute-start.7 = (bf16[1,184,128]{2,1,0:T(8,128)(2,1)}, bf16[1,184,128]{2,1,0:T(8,128)(2,1)S(1)}, u32[]{:S(2)}, u32[]{:S(2)}) collective-permute-start(bf16[1,184,128]{2,1,0:T(8,128)(2,1)} %refs_0_.1), channel_id=1, source_target_pairs={{0,8},{1,9},{2,10},{3,11},{4,12},{5,13},{6,14},{7,15},{8,0},{9,1},... | collective-permute-start | bytes 141320 | tf_op jit(solution)/shard_map/ppermute | solution.py:174
  3.8 2.5 %collective-permute-start = (bf16[1,184,128]{2,1,0:T(8,128)(2,1)}, bf16[1,184,128]{2,1,0:T(8,128)(2,1)S(1)}, u32[]{:S(2)}, u32[]{:S(2)}) collective-permute-start(bf16[1,184,128]{2,1,0:T(8,128)(2,1)} %refs_0_.1), channel_id=1, source_target_pairs={{0,24},{1,25},{2,26},{3,27},{4,28},{5,29},{6,30},{7,31},{8,16},{9,... | collective-permute-start | bytes 141320 | tf_op jit(solution)/shard_map/ppermute | solution.py:174
  6.2 0.1 collective-permute-start.1
  6.3 0.0 collective-permute-done.7.refs_1_
  6.4 0.8 %copy-done = bf16[1,184,128]{2,1,0:T(8,128)(2,1)S(1)} copy-done((bf16[1,184,128]{2,1,0:T(8,128)(2,1)S(1)}, bf16[1,184,128]{2,1,0:T(8,128)(2,1)}, u32[]{:S(2)}) %copy-start) | copy-done | bytes 47128
  7.2 0.1 norm.3.refs_0_
  7.3 2.6 %collective-permute-start.10 = (bf16[2,184,128]{2,1,0:T(8,128)(2,1)S(1)}, bf16[2,184,128]{2,1,0:T(8,128)(2,1)S(1)}, u32[]{:S(2)}, u32[]{:S(2)}) collective-permute-start(bf16[2,184,128]{2,1,0:T(8,128)(2,1)S(1)} %norm.3.refs_0_), channel_id=1, source_target_pairs={{0,6},{1,7},{2,4},{3,5},{4,2},{5,3},{6,0},{7,1},{8,14},{9,15},{10,... | collective-permute-start | bytes 282632 | tf_op jit(solution)/shard_map/ppermute | solution.py:174
  9.9 0.5 %collective-permute-start.8 = (bf16[2,184,128]{2,1,0:T(8,128)(2,1)S(1)}, bf16[2,184,128]{2,1,0:T(8,128)(2,1)S(1)}, u32[]{:S(2)}, u32[]{:S(2)}) collective-permute-start(bf16[2,184,128]{2,1,0:T(8,128)(2,1)S(1)} %norm.3.refs_0_), channel_id=1, source_target_pairs={{0,4},{1,5},{2,6},{3,7},{4,0},{5,1},{6,2},{7,3},{8,12},{9,13},{10,... | collective-permute-start | bytes 282632 | tf_op jit(solution)/shard_map/ppermute | solution.py:174
  10.4 0.4 %collective-permute-start.9 = (bf16[2,184,128]{2,1,0:T(8,128)(2,1)S(1)}, bf16[2,184,128]{2,1,0:T(8,128)(2,1)S(1)}, u32[]{:S(2)}, u32[]{:S(2)}) collective-permute-start(bf16[2,184,128]{2,1,0:T(8,128)(2,1)S(1)} %norm.3.refs_0_), channel_id=1, source_target_pairs={{0,2},{1,3},{2,0},{3,1},{4,6},{5,7},{6,4},{7,5},{8,10},{9,11},{10,... | collective-permute-start | bytes 282632 | tf_op jit(solution)/shard_map/ppermute | solution.py:174
  10.9 1.0 %collective-permute-done.1.refs_1_ = bf16[1,184,128]{2,1,0:T(8,128)(2,1)S(1)} collective-permute-done((bf16[1,184,128]{2,1,0:T(8,128)(2,1)}, bf16[1,184,128]{2,1,0:T(8,128)(2,1)S(1)}, u32[]{:S(2)}, u32[]{:S(2)}) %collective-permute-start.1) | collective-permute-done | bytes 47136 | tf_op jit(solution)/shard_map/ppermute | solution.py:174
  11.9 0.1 norm.2.refs_1_
  12.1 1.6 %collective-permute-start.4 = (bf16[2,184,128]{2,1,0:T(8,128)(2,1)S(1)}, bf16[2,184,128]{2,1,0:T(8,128)(2,1)S(1)}, u32[]{:S(2)}, u32[]{:S(2)}) collective-permute-start(bf16[2,184,128]{2,1,0:T(8,128)(2,1)S(1)} %norm.2.refs_1_), channel_id=1, source_target_pairs={{0,4},{1,5},{2,6},{3,7},{4,0},{5,1},{6,2},{7,3},{8,12},{9,13},{10,... | collective-permute-start | bytes 282632 | tf_op jit(solution)/shard_map/ppermute | solution.py:174
  13.6 1.5 %collective-permute-start.5 = (bf16[2,184,128]{2,1,0:T(8,128)(2,1)S(1)}, bf16[2,184,128]{2,1,0:T(8,128)(2,1)S(1)}, u32[]{:S(2)}, u32[]{:S(2)}) collective-permute-start(bf16[2,184,128]{2,1,0:T(8,128)(2,1)S(1)} %norm.2.refs_1_), channel_id=1, source_target_pairs={{0,2},{1,3},{2,0},{3,1},{4,6},{5,7},{6,4},{7,5},{8,10},{9,11},{10,... | collective-permute-start | bytes 282632 | tf_op jit(solution)/shard_map/ppermute | solution.py:174
  15.2 0.1 collective-permute-start.12
  15.2 0.2 collective-permute-done.8.refs_2_
  15.5 0.0 collective-permute-done.9.refs_3_
  15.5 0.3 %collective-permute-start.11 = (bf16[6,184,128]{2,1,0:T(8,128)(2,1)S(1)}, bf16[6,184,128]{2,1,0:T(8,128)(2,1)S(1)}, u32[]{:S(2)}, u32[]{:S(2)}) collective-permute-start(bf16[6,184,128]{2,1,0:T(8,128)(2,1)S(1)} %pad_maximum_fusion), channel_id=1, source_target_pairs={{0,1},{1,0},{2,3},{3,2},{4,5},{5,4},{6,7},{7,6},{8,9},{9,8},{10,11... | collective-permute-start | bytes 847880 | tf_op jit(solution)/shard_map/ppermute | solution.py:174
  15.8 0.8 %collective-permute-done.4.refs_1_ = bf16[2,184,128]{2,1,0:T(8,128)(2,1)S(1)} collective-permute-done((bf16[2,184,128]{2,1,0:T(8,128)(2,1)S(1)}, bf16[2,184,128]{2,1,0:T(8,128)(2,1)S(1)}, u32[]{:S(2)}, u32[]{:S(2)}) %collective-permute-start.4) | collective-permute-done | bytes 94240 | tf_op jit(solution)/shard_map/ppermute | solution.py:174
  16.7 1.5 %collective-permute-done.5.refs_2_ = bf16[2,184,128]{2,1,0:T(8,128)(2,1)S(1)} collective-permute-done((bf16[2,184,128]{2,1,0:T(8,128)(2,1)S(1)}, bf16[2,184,128]{2,1,0:T(8,128)(2,1)S(1)}, u32[]{:S(2)}, u32[]{:S(2)}) %collective-permute-start.5) | collective-permute-done | bytes 94240 | tf_op jit(solution)/shard_map/ppermute | solution.py:174
  18.2 0.0 copy-start.1
  18.2 0.0 copy-start.2
  18.2 0.1 collective-permute-start.6
  18.3 1.6 %collective-permute-start.2 = (bf16[2,184,128]{2,1,0:T(8,128)(2,1)S(1)}, bf16[2,184,128]{2,1,0:T(8,128)(2,1)S(1)}, u32[]{:S(2)}, u32[]{:S(2)}) collective-permute-start(bf16[2,184,128]{2,1,0:T(8,128)(2,1)S(1)} %norm.2.refs_1_), channel_id=1, source_target_pairs={{0,6},{1,7},{2,4},{3,5},{4,2},{5,3},{6,0},{7,1},{8,14},{9,15},{10,... | collective-permute-start | bytes 282632 | tf_op jit(solution)/shard_map/ppermute | solution.py:174
  19.9 4.5 %collective-permute-done.2.refs_0_ = bf16[2,184,128]{2,1,0:T(8,128)(2,1)S(1)} collective-permute-done((bf16[2,184,128]{2,1,0:T(8,128)(2,1)S(1)}, bf16[2,184,128]{2,1,0:T(8,128)(2,1)S(1)}, u32[]{:S(2)}, u32[]{:S(2)}) %collective-permute-start.2) | collective-permute-done | bytes 94240 | tf_op jit(solution)/shard_map/ppermute | solution.py:174
  24.3 0.0 copy-start.5
  24.4 0.6 %copy-done.4 = f32[4,12]{1,0:T(4,128)S(1)} copy-done((f32[4,12]{1,0:T(4,128)S(1)}, f32[4,12]{1,0:T(4,128)}, u32[]{:S(2)}) %copy-start.4) | copy-done | bytes 216
  25.0 0.4 %prep.1 = (f32[128,128]{1,0:T(8,128)S(1)}, bf16[128,128]{1,0:T(8,128)(2,1)S(1)}, f32[1,128]{1,0:T(1,128)S(1)}, f32[32,128]{1,0:T(8,128)S(1)}, f32[32,128]{1,0:T(8,128)S(1)}, /*index=5*/f32[2,128]{1,0:T(2,128)S(1)}) custom-call(s32[32,32]{1,0:T(8,128)S(1)} %order.1.order_ref, s32[16,12]{1,0:T(8,128)S(1)} %copy-done.2, s32[1,32]{1,0:T(1,128)S(1)} %bitcast.6, ...), custom_call_target="tpu_custom_call" | custom-call | tf_op jit(solution)/shard_map/prep/pallas_call | solution.py:317
  25.4 0.7 %shard_map.77 = (f32[2,128,128]{2,1,0:T(8,128)S(1)}, f32[2,128]{1,0:T(2,128)S(1)}) custom-call(bf16[2,184,128]{2,1,0:T(8,128)(2,1)S(1)} %norm.3.refs_0_, bf16[2,184,128]{2,1,0:T(8,128)(2,1)S(1)} %norm.2.refs_1_, bf16[2,184,128]{2,1,0:T(8,128)(2,1)S(1)} %collective-permute-done.8.refs_2_, bf16[2,184,128]{2,1,0:T(8,128)(2,1)S(1)} %collective-permute-done.9.refs_3_, ...), custom_call_target="tpu_custom_call" | custom-call | tf_op jit(solution)/shard_map/pallas_call | solution.py:341
  26.2 0.5 %shard_map.78 = (f32[2,128,128]{2,1,0:T(8,128)S(1)}, f32[2,128]{1,0:T(2,128)S(1)}) custom-call(bf16[4,184,128]{2,1,0:T(8,128)(2,1)S(1)} %collective-permute-done.12.refs_0_, bf16[128,128]{1,0:T(8,128)(2,1)S(1)} %get-tuple-element.18.refs_5_.refs_1_.refs_3_.refs_2_, f32[32,128]{1,0:T(8,128)S(1)} %get-tuple-element.19.refs_6_.refs_2_.refs_4_.refs_3_, ...), custom_call_target="tpu_custom_call" | custom-call | tf_op jit(solution)/shard_map/pallas_call | solution.py:341
  26.6 0.7 %shard_map.79 = (f32[2,128,128]{2,1,0:T(8,128)S(1)}, f32[2,128]{1,0:T(2,128)S(1)}) custom-call(bf16[6,184,128]{2,1,0:T(8,128)(2,1)S(1)} %collective-permute-done.11.refs_0_, bf16[2,184,128]{2,1,0:T(8,128)(2,1)S(1)} %collective-permute-done.4.refs_1_, bf16[2,184,128]{2,1,0:T(8,128)(2,1)S(1)} %collective-permute-done.5.refs_2_, ...), custom_call_target="tpu_custom_call" | custom-call | tf_op jit(solution)/shard_map/pallas_call | solution.py:341
  27.4 0.5 %shard_map.80 = (f32[2,128,128]{2,1,0:T(8,128)S(1)}, f32[2,128]{1,0:T(2,128)S(1)}) custom-call(bf16[2,184,128]{2,1,0:T(8,128)(2,1)S(1)} %collective-permute-done.2.refs_0_, bf16[4,184,128]{2,1,0:T(8,128)(2,1)S(1)} %collective-permute-done.6.refs_1_, bf16[128,128]{1,0:T(8,128)(2,1)S(1)} %get-tuple-element.18.refs_5_.refs_1_.refs_3_.refs_2_, ...), custom_call_target="tpu_custom_call" | custom-call | tf_op jit(solution)/shard_map/pallas_call | solution.py:341
  27.9 1.1 %shard_map.81 = (f32[128,128]{1,0:T(8,128)}, f32[1,4]{1,0:T(1,128)}) custom-call(bf16[2,184,128]{2,1,0:T(8,128)(2,1)S(1)} %collective-permute-done.3.refs_0_, bf16[128,128]{1,0:T(8,128)(2,1)S(1)} %get-tuple-element.18.refs_5_.refs_1_.refs_3_.refs_2_, f32[32,128]{1,0:T(8,128)S(1)} %get-tuple-element.19.refs_6_.refs_2_.refs_4_.refs_3_, ...), custom_call_target="tpu_custom_call" | custom-call | tf_op jit(solution)/shard_map/pallas_call | solution.py:341
  (18 shorter events, 0.1 us)
Async XLA Ops:
  0.6 5.7 %copy-start.3 = (s32[8]{0:T(128)S(1)}, s32[8]{0:T(128)}, u32[]{:S(2)}) copy-start(s32[8]{0:T(128)} %param.8) | copy-start | bytes 100
  0.6 5.7 %collective-permute-start.7 = (bf16[1,184,128]{2,1,0:T(8,128)(2,1)}, bf16[1,184,128]{2,1,0:T(8,128)(2,1)S(1)}, u32[]{:S(2)}, u32[]{:S(2)}) collective-permute-start(bf16[1,184,128]{2,1,0:T(8,128)(2,1)} %refs_0_.1), channel_id=1, source_target_pairs={{0,8},{1,9},{2,10},{3,11},{4,12},{5,13},{6,14},{7,15},{8,0},{9,1},... | collective-permute-start | bytes 141320 | tf_op jit(solution)/shard_map/ppermute | solution.py:174
  3.8 7.1 %collective-permute-start = (bf16[1,184,128]{2,1,0:T(8,128)(2,1)}, bf16[1,184,128]{2,1,0:T(8,128)(2,1)S(1)}, u32[]{:S(2)}, u32[]{:S(2)}) collective-permute-start(bf16[1,184,128]{2,1,0:T(8,128)(2,1)} %refs_0_.1), channel_id=1, source_target_pairs={{0,24},{1,25},{2,26},{3,27},{4,28},{5,29},{6,30},{7,31},{8,16},{9,... | collective-permute-start | bytes 141320 | tf_op jit(solution)/shard_map/ppermute | solution.py:174
  6.2 5.7 %collective-permute-start.1 = (bf16[1,184,128]{2,1,0:T(8,128)(2,1)}, bf16[1,184,128]{2,1,0:T(8,128)(2,1)S(1)}, u32[]{:S(2)}, u32[]{:S(2)}) collective-permute-start(bf16[1,184,128]{2,1,0:T(8,128)(2,1)} %refs_0_.1), channel_id=1, source_target_pairs={{0,16},{1,17},{2,18},{3,19},{4,20},{5,21},{6,22},{7,23},{8,24},{9,... | collective-permute-start | bytes 141320 | tf_op jit(solution)/shard_map/ppermute | solution.py:174
  6.4 0.8 %copy-start = (bf16[1,184,128]{2,1,0:T(8,128)(2,1)S(1)}, bf16[1,184,128]{2,1,0:T(8,128)(2,1)}, u32[]{:S(2)}) copy-start(bf16[1,184,128]{2,1,0:T(8,128)(2,1)} %refs_0_.1) | copy-start | bytes 141316
  7.3 7.8 %collective-permute-start.10 = (bf16[2,184,128]{2,1,0:T(8,128)(2,1)S(1)}, bf16[2,184,128]{2,1,0:T(8,128)(2,1)S(1)}, u32[]{:S(2)}, u32[]{:S(2)}) collective-permute-start(bf16[2,184,128]{2,1,0:T(8,128)(2,1)S(1)} %norm.3.refs_0_), channel_id=1, source_target_pairs={{0,6},{1,7},{2,4},{3,5},{4,2},{5,3},{6,0},{7,1},{8,14},{9,15},{10,... | collective-permute-start | bytes 282632 | tf_op jit(solution)/shard_map/ppermute | solution.py:174
  9.9 5.5 %collective-permute-start.8 = (bf16[2,184,128]{2,1,0:T(8,128)(2,1)S(1)}, bf16[2,184,128]{2,1,0:T(8,128)(2,1)S(1)}, u32[]{:S(2)}, u32[]{:S(2)}) collective-permute-start(bf16[2,184,128]{2,1,0:T(8,128)(2,1)S(1)} %norm.3.refs_0_), channel_id=1, source_target_pairs={{0,4},{1,5},{2,6},{3,7},{4,0},{5,1},{6,2},{7,3},{8,12},{9,13},{10,... | collective-permute-start | bytes 282632 | tf_op jit(solution)/shard_map/ppermute | solution.py:174
  10.4 5.0 %collective-permute-start.9 = (bf16[2,184,128]{2,1,0:T(8,128)(2,1)S(1)}, bf16[2,184,128]{2,1,0:T(8,128)(2,1)S(1)}, u32[]{:S(2)}, u32[]{:S(2)}) collective-permute-start(bf16[2,184,128]{2,1,0:T(8,128)(2,1)S(1)} %norm.3.refs_0_), channel_id=1, source_target_pairs={{0,2},{1,3},{2,0},{3,1},{4,6},{5,7},{6,4},{7,5},{8,10},{9,11},{10,... | collective-permute-start | bytes 282632 | tf_op jit(solution)/shard_map/ppermute | solution.py:174
  12.1 4.6 %collective-permute-start.4 = (bf16[2,184,128]{2,1,0:T(8,128)(2,1)S(1)}, bf16[2,184,128]{2,1,0:T(8,128)(2,1)S(1)}, u32[]{:S(2)}, u32[]{:S(2)}) collective-permute-start(bf16[2,184,128]{2,1,0:T(8,128)(2,1)S(1)} %norm.2.refs_1_), channel_id=1, source_target_pairs={{0,4},{1,5},{2,6},{3,7},{4,0},{5,1},{6,2},{7,3},{8,12},{9,13},{10,... | collective-permute-start | bytes 282632 | tf_op jit(solution)/shard_map/ppermute | solution.py:174
  13.6 4.6 %collective-permute-start.5 = (bf16[2,184,128]{2,1,0:T(8,128)(2,1)S(1)}, bf16[2,184,128]{2,1,0:T(8,128)(2,1)S(1)}, u32[]{:S(2)}, u32[]{:S(2)}) collective-permute-start(bf16[2,184,128]{2,1,0:T(8,128)(2,1)S(1)} %norm.2.refs_1_), channel_id=1, source_target_pairs={{0,2},{1,3},{2,0},{3,1},{4,6},{5,7},{6,4},{7,5},{8,10},{9,11},{10,... | collective-permute-start | bytes 282632 | tf_op jit(solution)/shard_map/ppermute | solution.py:174
  15.2 11.0 %collective-permute-start.12 = (bf16[4,184,128]{2,1,0:T(8,128)(2,1)S(1)}, bf16[4,184,128]{2,1,0:T(8,128)(2,1)S(1)}, u32[]{:S(2)}, u32[]{:S(2)}) collective-permute-start(bf16[4,184,128]{2,1,0:T(8,128)(2,1)S(1)} %pad_maximum_fusion.2), channel_id=1, source_target_pairs={{0,1},{1,0},{2,3},{3,2},{4,5},{5,4},{6,7},{7,6},{8,9},{9,8},{10,11... | collective-permute-start | bytes 565256 | tf_op jit(solution)/shard_map/ppermute | solution.py:174
  15.5 11.1 %collective-permute-start.11 = (bf16[6,184,128]{2,1,0:T(8,128)(2,1)S(1)}, bf16[6,184,128]{2,1,0:T(8,128)(2,1)S(1)}, u32[]{:S(2)}, u32[]{:S(2)}) collective-permute-start(bf16[6,184,128]{2,1,0:T(8,128)(2,1)S(1)} %pad_maximum_fusion), channel_id=1, source_target_pairs={{0,1},{1,0},{2,3},{3,2},{4,5},{5,4},{6,7},{7,6},{8,9},{9,8},{10,11... | collective-permute-start | bytes 847880 | tf_op jit(solution)/shard_map/ppermute | solution.py:174
  18.2 6.1 %copy-start.1 = (bf16[4,32,128]{2,1,0:T(8,128)(2,1)S(1)}, bf16[4,32,128]{2,1,0:T(8,128)(2,1)}, u32[]{:S(2)}) copy-start(bf16[4,32,128]{2,1,0:T(8,128)(2,1)} %query_ref.1) | copy-start | bytes 98308
  18.2 6.1 %copy-start.2 = (s32[16,12]{1,0:T(8,128)S(1)}, s32[16,12]{1,0:T(8,128)}, u32[]{:S(2)}) copy-start(s32[16,12]{1,0:T(8,128)} %cand_ref.1) | copy-start | bytes 2308
  18.2 9.1 %collective-permute-start.6 = (bf16[4,184,128]{2,1,0:T(8,128)(2,1)S(1)}, bf16[4,184,128]{2,1,0:T(8,128)(2,1)S(1)}, u32[]{:S(2)}, u32[]{:S(2)}) collective-permute-start(bf16[4,184,128]{2,1,0:T(8,128)(2,1)S(1)} %pad_maximum_fusion.1), channel_id=1, source_target_pairs={{0,1},{1,0},{2,3},{3,2},{4,5},{5,4},{6,7},{7,6},{8,9},{9,8},{10,11... | collective-permute-start | bytes 565256 | tf_op jit(solution)/shard_map/ppermute | solution.py:174
  18.3 6.0 %collective-permute-start.2 = (bf16[2,184,128]{2,1,0:T(8,128)(2,1)S(1)}, bf16[2,184,128]{2,1,0:T(8,128)(2,1)S(1)}, u32[]{:S(2)}, u32[]{:S(2)}) collective-permute-start(bf16[2,184,128]{2,1,0:T(8,128)(2,1)S(1)} %norm.2.refs_1_), channel_id=1, source_target_pairs={{0,6},{1,7},{2,4},{3,5},{4,2},{5,3},{6,0},{7,1},{8,14},{9,15},{10,... | collective-permute-start | bytes 282632 | tf_op jit(solution)/shard_map/ppermute | solution.py:174
  24.3 3.6 %collective-permute-start.3 = (bf16[2,184,128]{2,1,0:T(8,128)(2,1)S(1)}, bf16[2,184,128]{2,1,0:T(8,128)(2,1)S(1)}, u32[]{:S(2)}, u32[]{:S(2)}) collective-permute-start(bf16[2,184,128]{2,1,0:T(8,128)(2,1)S(1)} %collective-permute-done.2.refs_0_), channel_id=1, source_target_pairs={{0,1},{1,0},{2,3},{3,2},{4,5},{5,4},{6,7},{7,6},{8,9},{9,8},{10,11... | collective-permute-start | bytes 282632 | tf_op jit(solution)/shard_map/ppermute | solution.py:174
  24.3 0.7 %copy-start.4 = (f32[4,12]{1,0:T(4,128)S(1)}, f32[4,12]{1,0:T(4,128)}, u32[]{:S(2)}) copy-start(f32[4,12]{1,0:T(4,128)} %teacher_ref.1) | copy-start | bytes 580
  24.3 0.7 %copy-start.5 = (s32[32]{0:T(128)S(1)}, s32[32]{0:T(128)}, u32[]{:S(2)}) copy-start(s32[32]{0:T(128)} %param.10) | copy-start | bytes 388

commit v3 on v2

--- a/solution.py
+++ b/solution.py
@@ -40,8 +40,9 @@
     me = lax.axis_index("owner") * lax.axis_size("batch") + lax.axis_index("batch")
     place = lax.broadcasted_iota(jnp.int32, out_ref.shape, 0)
     row = jnp.zeros(out_ref.shape, jnp.int32)
+    odd = lax.axis_index("owner") % 2
     for number, delta in enumerate(order):
-        row = jnp.where(place == number, delta, row)
+        row = jnp.where(place == number, delta[0] + odd * (delta[1] - delta[0]), row)
     out_ref[...] = row ^ me
 
 
@@ -168,29 +169,32 @@
     div_ref[...] = exact_dot(div, pick)
 
 
-def exchange(piece, db, do):
+def exchange(piece, *ways):
     nb, no = lax.axis_size("batch"), lax.axis_size("owner")
-    pairs = [(b * no + o, (b ^ db) * no + (o ^ do)) for b in range(nb) for o in range(no)]
+    ways = ways * (2 // len(ways))
+    pairs = [(b * no + o, (b ^ ways[o % 2][0]) * no + (o ^ ways[o % 2][1])) for b in range(nb) for o in range(no)]
     value = lax.ppermute(piece[0], ("batch", "owner"), pairs)
-    return value, [d ^ db ^ nb * do for d in piece[1]]
+    even, odd = (db ^ nb * do for db, do in ways)
+    swapped = ways[0][1] % 2
+    return value, [(q ^ even, p ^ odd) if swapped else (p ^ even, q ^ odd) for p, q in piece[1]]
 
 
 def gather_pool(pool, normalize):
     nb = lax.axis_size("batch")
     masks = [2] + list(range(nb - 2, 2, -2))
-    raw = [exchange((pool, [0]), mask, 0)[0] for mask in masks]
+    raw = [exchange((pool, [(0, 0)]), (mask, 0))[0] for mask in masks]
     held = normalize([0, masks[0]], [pool, raw[0]])
     rest = normalize(masks[1:], raw[1:])
-    near = ((1, 0), (0, 2), (1, 2))
+    near = (((1, 2), (1, 0)), ((1, 0), (0, 2)), ((0, 2), (1, 2)))
     beside = [exchange(held, *way) for way in near]
     last = [exchange(rest, *way) for way in near]
     mine = [held, rest]
 
     def over(*pieces):
         value = jnp.concatenate([v for v, _ in pieces], axis=0) if len(pieces) > 1 else pieces[0][0]
-        return exchange((value, [d for _, o in pieces for d in o]), 0, 1)
-
-    return [[*mine, *beside], [over(*mine)], [over(*beside), *last[:2]], [last[2], over(*last[:2])], [over(last[2])]]
+        return exchange((value, [d for _, o in pieces for d in o]), (0, 1))
+
+    return [[*mine, *beside], [over(*mine), over(*beside)], last, [over(*last[:2])], [over(last[2])]]
 
 
 def unit_rows(values):
@@ -303,7 +307,7 @@
             out_specs=VMEM,
             name="norm",
         )(*in_vmem(lengths.reshape(1, -1), *blocks))
-        return value, list(masks)
+        return value, [(mask, mask) for mask in masks]
 
     stages = gather_pool(pool, normalize)
     order = [d for stage in stages for _, offs in stage for d in offs]

time: 29.3 us -> 29.9 us (1.020)
  waiting for transfers between devices: 8.08 us -> 9.94 us
  starting transfers between devices: 14.4 us -> 13.1 us
    ppermute x13, waiting for transfers between devices: 8.08 us -> 9.94 us  [exchange(): value = lax.ppermute(piece[0], ('batch', 'owner'), pairs)]
    ppermute x13, starting transfers between devices: 14.4 us -> 13.1 us  [exchange(): value = lax.ppermute(piece[0], ('batch', 'owner'), pairs)]
where the time goes in v3:
time: 29.9 us; the launch traced here: 29.7 us
  starting transfers between devices  13.1 us (44%)
  waiting for transfers between devices  9.94 us (33%)
  Pallas kernels  4.27 us (14%)
  local copies, waits for them, and re-layouts  1.47 us (5%)
  between operations  0.82 us (3%)
    ppermute x13, starting transfers between devices, exchange(): value = lax.ppermute(piece[0], ('batch', 'owner'), pairs)  13.1 us
    ppermute x13, waiting for transfers between devices, exchange(): value = lax.ppermute(piece[0], ('batch', 'owner'), pairs)  9.94 us
    pallas_call x5, Pallas kernels, local_all(): pl.pallas_call(functools.partial(score_kernel, counts, start, toks, numbe...  3.57 us
    unnamed x12, local copies, waits for them, and re-layouts  1.47 us
  transfers between devices with their start and end apart: 13, of which 5 were waited for; matrix products, arithmetic and copies ran while one was open for 0% of the time, Pallas kernels for 11%

profile of v3, /device:TPU:0, one launch (start us, length us, event | category | flops | bytes accessed | tf_op | source)
XLA Modules:
  0.0 29.7 jit_solution(17309037245331603171)
XLA Ops:
  0.6 3.1 %collective-permute-start.7 = (bf16[1,184,128]{2,1,0:T(8,128)(2,1)}, bf16[1,184,128]{2,1,0:T(8,128)(2,1)S(1)}, u32[]{:S(2)}, u32[]{:S(2)}) collective-permute-start(bf16[1,184,128]{2,1,0:T(8,128)(2,1)} %refs_0_.1), channel_id=1, source_target_pairs={{0,8},{1,9},{2,10},{3,11},{4,12},{5,13},{6,14},{7,15},{8,0},{9,1},... | collective-permute-start | bytes 141320 | tf_op jit(solution)/shard_map/ppermute | solution.py:176
  3.8 2.5 %collective-permute-start = (bf16[1,184,128]{2,1,0:T(8,128)(2,1)}, bf16[1,184,128]{2,1,0:T(8,128)(2,1)S(1)}, u32[]{:S(2)}, u32[]{:S(2)}) collective-permute-start(bf16[1,184,128]{2,1,0:T(8,128)(2,1)} %refs_0_.1), channel_id=1, source_target_pairs={{0,24},{1,25},{2,26},{3,27},{4,28},{5,29},{6,30},{7,31},{8,16},{9,... | collective-permute-start | bytes 141320 | tf_op jit(solution)/shard_map/ppermute | solution.py:176
  6.2 0.1 collective-permute-start.1
  6.3 0.0 collective-permute-done.7.refs_1_
  6.4 0.8 %copy-done = bf16[1,184,128]{2,1,0:T(8,128)(2,1)S(1)} copy-done((bf16[1,184,128]{2,1,0:T(8,128)(2,1)S(1)}, bf16[1,184,128]{2,1,0:T(8,128)(2,1)}, u32[]{:S(2)}) %copy-start) | copy-done | bytes 47128
  7.2 0.1 norm.3.refs_0_
  7.3 1.6 %collective-permute-start.10 = (bf16[2,184,128]{2,1,0:T(8,128)(2,1)S(1)}, bf16[2,184,128]{2,1,0:T(8,128)(2,1)S(1)}, u32[]{:S(2)}, u32[]{:S(2)}) collective-permute-start(bf16[2,184,128]{2,1,0:T(8,128)(2,1)S(1)} %norm.3.refs_0_), channel_id=1, source_target_pairs={{0,4},{1,3},{2,6},{3,1},{4,0},{5,7},{6,2},{7,5},{8,12},{9,11},{10,... | collective-permute-start | bytes 282632 | tf_op jit(solution)/shard_map/ppermute | solution.py:176
  9.0 1.5 %collective-permute-start.11 = (bf16[2,184,128]{2,1,0:T(8,128)(2,1)S(1)}, bf16[2,184,128]{2,1,0:T(8,128)(2,1)S(1)}, u32[]{:S(2)}, u32[]{:S(2)}) collective-permute-start(bf16[2,184,128]{2,1,0:T(8,128)(2,1)S(1)} %norm.3.refs_0_), channel_id=1, source_target_pairs={{0,2},{1,7},{2,0},{3,5},{4,6},{5,3},{6,4},{7,1},{8,10},{9,15},{10,... | collective-permute-start | bytes 282632 | tf_op jit(solution)/shard_map/ppermute | solution.py:176
  10.5 0.4 %collective-permute-start.9 = (bf16[2,184,128]{2,1,0:T(8,128)(2,1)S(1)}, bf16[2,184,128]{2,1,0:T(8,128)(2,1)S(1)}, u32[]{:S(2)}, u32[]{:S(2)}) collective-permute-start(bf16[2,184,128]{2,1,0:T(8,128)(2,1)S(1)} %norm.3.refs_0_), channel_id=1, source_target_pairs={{0,6},{1,5},{2,4},{3,7},{4,2},{5,1},{6,0},{7,3},{8,14},{9,13},{10,... | collective-permute-start | bytes 282632 | tf_op jit(solution)/shard_map/ppermute | solution.py:176
  10.9 1.0 %collective-permute-done.1.refs_1_ = bf16[1,184,128]{2,1,0:T(8,128)(2,1)S(1)} collective-permute-done((bf16[1,184,128]{2,1,0:T(8,128)(2,1)}, bf16[1,184,128]{2,1,0:T(8,128)(2,1)S(1)}, u32[]{:S(2)}, u32[]{:S(2)}) %collective-permute-start.1) | collective-permute-done | bytes 47136 | tf_op jit(solution)/shard_map/ppermute | solution.py:176
  11.9 0.1 norm.2.refs_1_
  12.1 2.5 %collective-permute-start.4 = (bf16[2,184,128]{2,1,0:T(8,128)(2,1)S(1)}, bf16[2,184,128]{2,1,0:T(8,128)(2,1)S(1)}, u32[]{:S(2)}, u32[]{:S(2)}) collective-permute-start(bf16[2,184,128]{2,1,0:T(8,128)(2,1)S(1)} %norm.2.refs_1_), channel_id=1, source_target_pairs={{0,6},{1,5},{2,4},{3,7},{4,2},{5,1},{6,0},{7,3},{8,14},{9,13},{10,... | collective-permute-start | bytes 282632 | tf_op jit(solution)/shard_map/ppermute | solution.py:176
  14.6 0.5 %collective-permute-start.5 = (bf16[2,184,128]{2,1,0:T(8,128)(2,1)S(1)}, bf16[2,184,128]{2,1,0:T(8,128)(2,1)S(1)}, u32[]{:S(2)}, u32[]{:S(2)}) collective-permute-start(bf16[2,184,128]{2,1,0:T(8,128)(2,1)S(1)} %norm.2.refs_1_), channel_id=1, source_target_pairs={{0,4},{1,3},{2,6},{3,1},{4,0},{5,7},{6,2},{7,5},{8,12},{9,11},{10,... | collective-permute-start | bytes 282632 | tf_op jit(solution)/shard_map/ppermute | solution.py:176
  15.1 0.1 collective-permute-start.8
  15.2 1.3 %collective-permute-done.9.refs_2_ = bf16[2,184,128]{2,1,0:T(8,128)(2,1)S(1)} collective-permute-done((bf16[2,184,128]{2,1,0:T(8,128)(2,1)S(1)}, bf16[2,184,128]{2,1,0:T(8,128)(2,1)S(1)}, u32[]{:S(2)}, u32[]{:S(2)}) %collective-permute-start.9) | collective-permute-done | bytes 94240 | tf_op jit(solution)/shard_map/ppermute | solution.py:176
  16.6 0.1 collective-permute-start.12
  16.7 0.9 %collective-permute-done.4.refs_0_ = bf16[2,184,128]{2,1,0:T(8,128)(2,1)S(1)} collective-permute-done((bf16[2,184,128]{2,1,0:T(8,128)(2,1)S(1)}, bf16[2,184,128]{2,1,0:T(8,128)(2,1)S(1)}, u32[]{:S(2)}, u32[]{:S(2)}) %collective-permute-start.4) | collective-permute-done | bytes 94240 | tf_op jit(solution)/shard_map/ppermute | solution.py:176
  17.6 1.5 %collective-permute-done.5.refs_1_ = bf16[2,184,128]{2,1,0:T(8,128)(2,1)S(1)} collective-permute-done((bf16[2,184,128]{2,1,0:T(8,128)(2,1)S(1)}, bf16[2,184,128]{2,1,0:T(8,128)(2,1)S(1)}, u32[]{:S(2)}, u32[]{:S(2)}) %collective-permute-start.5) | collective-permute-done | bytes 94240 | tf_op jit(solution)/shard_map/ppermute | solution.py:176
  19.2 0.0 copy-start.1
  19.2 0.0 copy-start.2
  19.2 0.1 collective-permute-start.6
  19.3 0.6 %collective-permute-start.2 = (bf16[2,184,128]{2,1,0:T(8,128)(2,1)S(1)}, bf16[2,184,128]{2,1,0:T(8,128)(2,1)S(1)}, u32[]{:S(2)}, u32[]{:S(2)}) collective-permute-start(bf16[2,184,128]{2,1,0:T(8,128)(2,1)S(1)} %norm.2.refs_1_), channel_id=1, source_target_pairs={{0,2},{1,7},{2,0},{3,5},{4,6},{5,3},{6,4},{7,1},{8,10},{9,15},{10,... | collective-permute-start | bytes 282632 | tf_op jit(solution)/shard_map/ppermute | solution.py:176
  19.8 5.1 %collective-permute-done.2.refs_2_ = bf16[2,184,128]{2,1,0:T(8,128)(2,1)S(1)} collective-permute-done((bf16[2,184,128]{2,1,0:T(8,128)(2,1)S(1)}, bf16[2,184,128]{2,1,0:T(8,128)(2,1)S(1)}, u32[]{:S(2)}, u32[]{:S(2)}) %collective-permute-start.2) | collective-permute-done | bytes 94240 | tf_op jit(solution)/shard_map/ppermute | solution.py:176
  24.9 0.0 copy-start.5
  25.0 0.6 %copy-done.4 = f32[4,12]{1,0:T(4,128)S(1)} copy-done((f32[4,12]{1,0:T(4,128)S(1)}, f32[4,12]{1,0:T(4,128)}, u32[]{:S(2)}) %copy-start.4) | copy-done | bytes 216
  25.6 0.0 copy-done.5
  25.6 0.4 %prep.1 = (f32[128,128]{1,0:T(8,128)S(1)}, bf16[128,128]{1,0:T(8,128)(2,1)S(1)}, f32[1,128]{1,0:T(1,128)S(1)}, f32[32,128]{1,0:T(8,128)S(1)}, f32[32,128]{1,0:T(8,128)S(1)}, /*index=5*/f32[2,128]{1,0:T(2,128)S(1)}) custom-call(s32[32,32]{1,0:T(8,128)S(1)} %order.1.order_ref, s32[16,12]{1,0:T(8,128)S(1)} %copy-done.2, s32[1,32]{1,0:T(1,128)S(1)} %bitcast.6, ...), custom_call_target="tpu_custom_call" | custom-call | tf_op jit(solution)/shard_map/prep/pallas_call | solution.py:321
  26.0 0.7 %shard_map.77 = (f32[2,128,128]{2,1,0:T(8,128)S(1)}, f32[2,128]{1,0:T(2,128)S(1)}) custom-call(bf16[2,184,128]{2,1,0:T(8,128)(2,1)S(1)} %norm.3.refs_0_, bf16[2,184,128]{2,1,0:T(8,128)(2,1)S(1)} %norm.2.refs_1_, bf16[2,184,128]{2,1,0:T(8,128)(2,1)S(1)} %collective-permute-done.9.refs_2_, bf16[2,184,128]{2,1,0:T(8,128)(2,1)S(1)} %collective-permute-done.10.refs_3_, ...), custom_call_target="tpu_custom_call" | custom-call | tf_op jit(solution)/shard_map/pallas_call | solution.py:345
  26.8 0.7 %shard_map.78 = (f32[2,128,128]{2,1,0:T(8,128)S(1)}, f32[2,128]{1,0:T(2,128)S(1)}) custom-call(bf16[4,184,128]{2,1,0:T(8,128)(2,1)S(1)} %collective-permute-done.8.refs_0_, bf16[6,184,128]{2,1,0:T(8,128)(2,1)S(1)} %collective-permute-done.12.refs_1_, bf16[128,128]{1,0:T(8,128)(2,1)S(1)} %get-tuple-element.18.refs_5_.refs_2_.refs_3_.refs_1_, ...), custom_call_target="tpu_custom_call" | custom-call | tf_op jit(solution)/shard_map/pallas_call | solution.py:345
  27.5 0.5 %shard_map.79 = (f32[2,128,128]{2,1,0:T(8,128)S(1)}, f32[2,128]{1,0:T(2,128)S(1)}) custom-call(bf16[2,184,128]{2,1,0:T(8,128)(2,1)S(1)} %collective-permute-done.4.refs_0_, bf16[2,184,128]{2,1,0:T(8,128)(2,1)S(1)} %collective-permute-done.5.refs_1_, bf16[2,184,128]{2,1,0:T(8,128)(2,1)S(1)} %collective-permute-done.2.refs_2_, ...), custom_call_target="tpu_custom_call" | custom-call | tf_op jit(solution)/shard_map/pallas_call | solution.py:345
  28.0 0.5 %shard_map.80 = (f32[2,128,128]{2,1,0:T(8,128)S(1)}, f32[2,128]{1,0:T(2,128)S(1)}) custom-call(bf16[4,184,128]{2,1,0:T(8,128)(2,1)S(1)} %collective-permute-done.6.refs_0_, bf16[128,128]{1,0:T(8,128)(2,1)S(1)} %get-tuple-element.18.refs_5_.refs_2_.refs_3_.refs_1_, f32[32,128]{1,0:T(8,128)S(1)} %get-tuple-element.19.refs_6_.refs_3_.refs_4_.refs_2_, ...), custom_call_target="tpu_custom_call" | custom-call | tf_op jit(solution)/shard_map/pallas_call | solution.py:345
  28.5 1.1 %shard_map.81 = (f32[128,128]{1,0:T(8,128)}, f32[1,4]{1,0:T(1,128)}) custom-call(bf16[2,184,128]{2,1,0:T(8,128)(2,1)S(1)} %collective-permute-done.3.refs_0_, bf16[128,128]{1,0:T(8,128)(2,1)S(1)} %get-tuple-element.18.refs_5_.refs_2_.refs_3_.refs_1_, f32[32,128]{1,0:T(8,128)S(1)} %get-tuple-element.19.refs_6_.refs_3_.refs_4_.refs_2_, ...), custom_call_target="tpu_custom_call" | custom-call | tf_op jit(solution)/shard_map/pallas_call | solution.py:345
  (18 shorter events, 0.1 us)
Async XLA Ops:
  0.6 5.7 %copy-start.3 = (s32[8]{0:T(128)S(1)}, s32[8]{0:T(128)}, u32[]{:S(2)}) copy-start(s32[8]{0:T(128)} %param.8) | copy-start | bytes 100
  0.6 5.7 %collective-permute-start.7 = (bf16[1,184,128]{2,1,0:T(8,128)(2,1)}, bf16[1,184,128]{2,1,0:T(8,128)(2,1)S(1)}, u32[]{:S(2)}, u32[]{:S(2)}) collective-permute-start(bf16[1,184,128]{2,1,0:T(8,128)(2,1)} %refs_0_.1), channel_id=1, source_target_pairs={{0,8},{1,9},{2,10},{3,11},{4,12},{5,13},{6,14},{7,15},{8,0},{9,1},... | collective-permute-start | bytes 141320 | tf_op jit(solution)/shard_map/ppermute | solution.py:176
  3.8 7.1 %collective-permute-start = (bf16[1,184,128]{2,1,0:T(8,128)(2,1)}, bf16[1,184,128]{2,1,0:T(8,128)(2,1)S(1)}, u32[]{:S(2)}, u32[]{:S(2)}) collective-permute-start(bf16[1,184,128]{2,1,0:T(8,128)(2,1)} %refs_0_.1), channel_id=1, source_target_pairs={{0,24},{1,25},{2,26},{3,27},{4,28},{5,29},{6,30},{7,31},{8,16},{9,... | collective-permute-start | bytes 141320 | tf_op jit(solution)/shard_map/ppermute | solution.py:176
  6.2 5.7 %collective-permute-start.1 = (bf16[1,184,128]{2,1,0:T(8,128)(2,1)}, bf16[1,184,128]{2,1,0:T(8,128)(2,1)S(1)}, u32[]{:S(2)}, u32[]{:S(2)}) collective-permute-start(bf16[1,184,128]{2,1,0:T(8,128)(2,1)} %refs_0_.1), channel_id=1, source_target_pairs={{0,16},{1,17},{2,18},{3,19},{4,20},{5,21},{6,22},{7,23},{8,24},{9,... | collective-permute-start | bytes 141320 | tf_op jit(solution)/shard_map/ppermute | solution.py:176
  6.4 0.8 %copy-start = (bf16[1,184,128]{2,1,0:T(8,128)(2,1)S(1)}, bf16[1,184,128]{2,1,0:T(8,128)(2,1)}, u32[]{:S(2)}) copy-start(bf16[1,184,128]{2,1,0:T(8,128)(2,1)} %refs_0_.1) | copy-start | bytes 141316
  7.3 7.8 %collective-permute-start.10 = (bf16[2,184,128]{2,1,0:T(8,128)(2,1)S(1)}, bf16[2,184,128]{2,1,0:T(8,128)(2,1)S(1)}, u32[]{:S(2)}, u32[]{:S(2)}) collective-permute-start(bf16[2,184,128]{2,1,0:T(8,128)(2,1)S(1)} %norm.3.refs_0_), channel_id=1, source_target_pairs={{0,4},{1,3},{2,6},{3,1},{4,0},{5,7},{6,2},{7,5},{8,12},{9,11},{10,... | collective-permute-start | bytes 282632 | tf_op jit(solution)/shard_map/ppermute | solution.py:176
  9.0 6.3 %collective-permute-start.11 = (bf16[2,184,128]{2,1,0:T(8,128)(2,1)S(1)}, bf16[2,184,128]{2,1,0:T(8,128)(2,1)S(1)}, u32[]{:S(2)}, u32[]{:S(2)}) collective-permute-start(bf16[2,184,128]{2,1,0:T(8,128)(2,1)S(1)} %norm.3.refs_0_), channel_id=1, source_target_pairs={{0,2},{1,7},{2,0},{3,5},{4,6},{5,3},{6,4},{7,1},{8,10},{9,15},{10,... | collective-permute-start | bytes 282632 | tf_op jit(solution)/shard_map/ppermute | solution.py:176
  10.5 6.1 %collective-permute-start.9 = (bf16[2,184,128]{2,1,0:T(8,128)(2,1)S(1)}, bf16[2,184,128]{2,1,0:T(8,128)(2,1)S(1)}, u32[]{:S(2)}, u32[]{:S(2)}) collective-permute-start(bf16[2,184,128]{2,1,0:T(8,128)(2,1)S(1)} %norm.3.refs_0_), channel_id=1, source_target_pairs={{0,6},{1,5},{2,4},{3,7},{4,2},{5,1},{6,0},{7,3},{8,14},{9,13},{10,... | collective-permute-start | bytes 282632 | tf_op jit(solution)/shard_map/ppermute | solution.py:176
  12.1 5.5 %collective-permute-start.4 = (bf16[2,184,128]{2,1,0:T(8,128)(2,1)S(1)}, bf16[2,184,128]{2,1,0:T(8,128)(2,1)S(1)}, u32[]{:S(2)}, u32[]{:S(2)}) collective-permute-start(bf16[2,184,128]{2,1,0:T(8,128)(2,1)S(1)} %norm.2.refs_1_), channel_id=1, source_target_pairs={{0,6},{1,5},{2,4},{3,7},{4,2},{5,1},{6,0},{7,3},{8,14},{9,13},{10,... | collective-permute-start | bytes 282632 | tf_op jit(solution)/shard_map/ppermute | solution.py:176
  14.6 4.6 %collective-permute-start.5 = (bf16[2,184,128]{2,1,0:T(8,128)(2,1)S(1)}, bf16[2,184,128]{2,1,0:T(8,128)(2,1)S(1)}, u32[]{:S(2)}, u32[]{:S(2)}) collective-permute-start(bf16[2,184,128]{2,1,0:T(8,128)(2,1)S(1)} %norm.2.refs_1_), channel_id=1, source_target_pairs={{0,4},{1,3},{2,6},{3,1},{4,0},{5,7},{6,2},{7,5},{8,12},{9,11},{10,... | collective-permute-start | bytes 282632 | tf_op jit(solution)/shard_map/ppermute | solution.py:176
  15.1 11.6 %collective-permute-start.8 = (bf16[4,184,128]{2,1,0:T(8,128)(2,1)S(1)}, bf16[4,184,128]{2,1,0:T(8,128)(2,1)S(1)}, u32[]{:S(2)}, u32[]{:S(2)}) collective-permute-start(bf16[4,184,128]{2,1,0:T(8,128)(2,1)S(1)} %pad_maximum_fusion.2), channel_id=1, source_target_pairs={{0,1},{1,0},{2,3},{3,2},{4,5},{5,4},{6,7},{7,6},{8,9},{9,8},{10,11... | collective-permute-start | bytes 565256 | tf_op jit(solution)/shard_map/ppermute | solution.py:176
  16.6 10.2 %collective-permute-start.12 = (bf16[6,184,128]{2,1,0:T(8,128)(2,1)S(1)}, bf16[6,184,128]{2,1,0:T(8,128)(2,1)S(1)}, u32[]{:S(2)}, u32[]{:S(2)}) collective-permute-start(bf16[6,184,128]{2,1,0:T(8,128)(2,1)S(1)} %pad_maximum_fusion), channel_id=1, source_target_pairs={{0,1},{1,0},{2,3},{3,2},{4,5},{5,4},{6,7},{7,6},{8,9},{9,8},{10,11... | collective-permute-start | bytes 847880 | tf_op jit(solution)/shard_map/ppermute | solution.py:176
  19.2 5.8 %copy-start.1 = (bf16[4,32,128]{2,1,0:T(8,128)(2,1)S(1)}, bf16[4,32,128]{2,1,0:T(8,128)(2,1)}, u32[]{:S(2)}) copy-start(bf16[4,32,128]{2,1,0:T(8,128)(2,1)} %query_ref.1) | copy-start | bytes 98308
  19.2 5.8 %copy-start.2 = (s32[16,12]{1,0:T(8,128)S(1)}, s32[16,12]{1,0:T(8,128)}, u32[]{:S(2)}) copy-start(s32[16,12]{1,0:T(8,128)} %cand_ref.1) | copy-start | bytes 2308
  19.2 8.9 %collective-permute-start.6 = (bf16[4,184,128]{2,1,0:T(8,128)(2,1)S(1)}, bf16[4,184,128]{2,1,0:T(8,128)(2,1)S(1)}, u32[]{:S(2)}, u32[]{:S(2)}) collective-permute-start(bf16[4,184,128]{2,1,0:T(8,128)(2,1)S(1)} %pad_maximum_fusion.1), channel_id=1, source_target_pairs={{0,1},{1,0},{2,3},{3,2},{4,5},{5,4},{6,7},{7,6},{8,9},{9,8},{10,11... | collective-permute-start | bytes 565256 | tf_op jit(solution)/shard_map/ppermute | solution.py:176
  19.3 5.6 %collective-permute-start.2 = (bf16[2,184,128]{2,1,0:T(8,128)(2,1)S(1)}, bf16[2,184,128]{2,1,0:T(8,128)(2,1)S(1)}, u32[]{:S(2)}, u32[]{:S(2)}) collective-permute-start(bf16[2,184,128]{2,1,0:T(8,128)(2,1)S(1)} %norm.2.refs_1_), channel_id=1, source_target_pairs={{0,2},{1,7},{2,0},{3,5},{4,6},{5,3},{6,4},{7,1},{8,10},{9,15},{10,... | collective-permute-start | bytes 282632 | tf_op jit(solution)/shard_map/ppermute | solution.py:176
  24.9 3.6 %collective-permute-start.3 = (bf16[2,184,128]{2,1,0:T(8,128)(2,1)S(1)}, bf16[2,184,128]{2,1,0:T(8,128)(2,1)S(1)}, u32[]{:S(2)}, u32[]{:S(2)}) collective-permute-start(bf16[2,184,128]{2,1,0:T(8,128)(2,1)S(1)} %collective-permute-done.2.refs_2_), channel_id=1, source_target_pairs={{0,1},{1,0},{2,3},{3,2},{4,5},{5,4},{6,7},{7,6},{8,9},{9,8},{10,11... | collective-permute-start | bytes 282632 | tf_op jit(solution)/shard_map/ppermute | solution.py:176
  24.9 0.7 %copy-start.4 = (f32[4,12]{1,0:T(4,128)S(1)}, f32[4,12]{1,0:T(4,128)}, u32[]{:S(2)}) copy-start(f32[4,12]{1,0:T(4,128)} %teacher_ref.1) | copy-start | bytes 580
  24.9 0.7 %copy-start.5 = (s32[32]{0:T(128)S(1)}, s32[32]{0:T(128)}, u32[]{:S(2)}) copy-start(s32[32]{0:T(128)} %param.10) | copy-start | bytes 388

commit v4 on v3

--- a/solution.py
+++ b/solution.py
@@ -185,8 +185,9 @@
     raw = [exchange((pool, [(0, 0)]), (mask, 0))[0] for mask in masks]
     held = normalize([0, masks[0]], [pool, raw[0]])
     rest = normalize(masks[1:], raw[1:])
-    near = (((1, 2), (1, 0)), ((1, 0), (0, 2)), ((0, 2), (1, 2)))
-    beside = [exchange(held, *way) for way in near]
+    near = (((1, 2), (0, 2)), ((1, 0), (1, 0)), ((0, 2), (1, 2)))
+    plain = (((1, 0),), ((0, 2),), ((1, 2),))
+    beside = [exchange(held, *way) for way in plain]
     last = [exchange(rest, *way) for way in near]
     mine = [held, rest]
 
@@ -194,7 +195,7 @@
         value = jnp.concatenate([v for v, _ in pieces], axis=0) if len(pieces) > 1 else pieces[0][0]
         return exchange((value, [d for _, o in pieces for d in o]), (0, 1))
 
-    return [[*mine, *beside], [over(*mine), over(*beside)], last, [over(*last[:2])], [over(last[2])]]
+    return [[*mine, *beside], [over(*mine), over(*beside)], last, [over(*last[:2]), over(last[2])]]
 
 
 def unit_rows(values):

time: 29.9 us -> 24.5 us (0.82)
  waiting for transfers between devices: 9.94 us -> 4.41 us
  starting transfers between devices: 13.1 us -> 13.5 us
  Pallas kernels: 4.27 us -> 3.96 us
    ppermute x13, waiting for transfers between devices: 9.94 us -> 4.41 us  [exchange(): value = lax.ppermute(piece[0], ('batch', 'owner'), pairs)]
    ppermute x13, starting transfers between devices: 13.1 us -> 13.5 us  [exchange(): value = lax.ppermute(piece[0], ('batch', 'owner'), pairs)]
    pallas_call x5 -> x4, Pallas kernels: 3.57 us -> 3.26 us  [local_all(): pl.pallas_call(functools.partial(score_kernel, counts, start, toks, numbe...]
  transfers between devices with their start and end apart: 13 -> 13, of which waited for: 5 -> 4; matrix products, arithmetic and copies ran while one was open for 0% -> 0% of each run, Pallas kernels for 11% -> 11%
where the time goes in v4:
time: 24.5 us; the launch traced here: 24.2 us
  starting transfers between devices  13.5 us (55%)
  waiting for transfers between devices  4.41 us (18%)
  Pallas kernels  3.96 us (16%)
  local copies, waits for them, and re-layouts  1.49 us (6%)
  between operations  0.78 us (3%)
    ppermute x13, starting transfers between devices, exchange(): value = lax.ppermute(piece[0], ('batch', 'owner'), pairs)  13.5 us
    ppermute x13, waiting for transfers between devices, exchange(): value = lax.ppermute(piece[0], ('batch', 'owner'), pairs)  4.41 us
    pallas_call x4, Pallas kernels, local_all(): pl.pallas_call(functools.partial(score_kernel, counts, start, toks, numbe...  3.26 us
    unnamed x12, local copies, waits for them, and re-layouts  1.49 us
  transfers between devices with their start and end apart: 13, of which 4 were waited for; matrix products, arithmetic and copies ran while one was open for 0% of the time, Pallas kernels for 11%

profile of v4, /device:TPU:0, one launch (start us, length us, event | category | flops | bytes accessed | tf_op | source)
XLA Modules:
  0.0 24.2 jit_solution(9783406509361402552)
XLA Ops:
  0.6 3.1 %collective-permute-start.7 = (bf16[1,184,128]{2,1,0:T(8,128)(2,1)}, bf16[1,184,128]{2,1,0:T(8,128)(2,1)S(1)}, u32[]{:S(2)}, u32[]{:S(2)}) collective-permute-start(bf16[1,184,128]{2,1,0:T(8,128)(2,1)} %refs_0_.1), channel_id=1, source_target_pairs={{0,8},{1,9},{2,10},{3,11},{4,12},{5,13},{6,14},{7,15},{8,0},{9,1},... | collective-permute-start | bytes 141320 | tf_op jit(solution)/shard_map/ppermute | solution.py:176
  3.8 2.5 %collective-permute-start = (bf16[1,184,128]{2,1,0:T(8,128)(2,1)}, bf16[1,184,128]{2,1,0:T(8,128)(2,1)S(1)}, u32[]{:S(2)}, u32[]{:S(2)}) collective-permute-start(bf16[1,184,128]{2,1,0:T(8,128)(2,1)} %refs_0_.1), channel_id=1, source_target_pairs={{0,24},{1,25},{2,26},{3,27},{4,28},{5,29},{6,30},{7,31},{8,16},{9,... | collective-permute-start | bytes 141320 | tf_op jit(solution)/shard_map/ppermute | solution.py:176
  6.2 0.1 collective-permute-start.1
  6.3 0.0 collective-permute-done.7.refs_1_
  6.4 0.8 %copy-done = bf16[1,184,128]{2,1,0:T(8,128)(2,1)S(1)} copy-done((bf16[1,184,128]{2,1,0:T(8,128)(2,1)S(1)}, bf16[1,184,128]{2,1,0:T(8,128)(2,1)}, u32[]{:S(2)}) %copy-start) | copy-done | bytes 47128
  7.2 0.1 norm.3.refs_0_
  7.3 1.7 %collective-permute-start.10 = (bf16[2,184,128]{2,1,0:T(8,128)(2,1)S(1)}, bf16[2,184,128]{2,1,0:T(8,128)(2,1)S(1)}, u32[]{:S(2)}, u32[]{:S(2)}) collective-permute-start(bf16[2,184,128]{2,1,0:T(8,128)(2,1)S(1)} %norm.3.refs_0_), channel_id=1, source_target_pairs={{0,2},{1,3},{2,0},{3,1},{4,6},{5,7},{6,4},{7,5},{8,10},{9,11},{10,... | collective-permute-start | bytes 282632 | tf_op jit(solution)/shard_map/ppermute | solution.py:176
  9.0 1.4 %collective-permute-start.11 = (bf16[2,184,128]{2,1,0:T(8,128)(2,1)S(1)}, bf16[2,184,128]{2,1,0:T(8,128)(2,1)S(1)}, u32[]{:S(2)}, u32[]{:S(2)}) collective-permute-start(bf16[2,184,128]{2,1,0:T(8,128)(2,1)S(1)} %norm.3.refs_0_), channel_id=1, source_target_pairs={{0,6},{1,7},{2,4},{3,5},{4,2},{5,3},{6,0},{7,1},{8,14},{9,15},{10,... | collective-permute-start | bytes 282632 | tf_op jit(solution)/shard_map/ppermute | solution.py:176
  10.4 0.5 %collective-permute-start.9 = (bf16[2,184,128]{2,1,0:T(8,128)(2,1)S(1)}, bf16[2,184,128]{2,1,0:T(8,128)(2,1)S(1)}, u32[]{:S(2)}, u32[]{:S(2)}) collective-permute-start(bf16[2,184,128]{2,1,0:T(8,128)(2,1)S(1)} %norm.3.refs_0_), channel_id=1, source_target_pairs={{0,4},{1,5},{2,6},{3,7},{4,0},{5,1},{6,2},{7,3},{8,12},{9,13},{10,... | collective-permute-start | bytes 282632 | tf_op jit(solution)/shard_map/ppermute | solution.py:176
  10.9 1.0 %collective-permute-done.1.refs_1_ = bf16[1,184,128]{2,1,0:T(8,128)(2,1)S(1)} collective-permute-done((bf16[1,184,128]{2,1,0:T(8,128)(2,1)}, bf16[1,184,128]{2,1,0:T(8,128)(2,1)S(1)}, u32[]{:S(2)}, u32[]{:S(2)}) %collective-permute-start.1) | collective-permute-done | bytes 47136 | tf_op jit(solution)/shard_map/ppermute | solution.py:176
  11.9 0.1 norm.2.refs_1_
  12.1 2.5 %collective-permute-start.2 = (bf16[2,184,128]{2,1,0:T(8,128)(2,1)S(1)}, bf16[2,184,128]{2,1,0:T(8,128)(2,1)S(1)}, u32[]{:S(2)}, u32[]{:S(2)}) collective-permute-start(bf16[2,184,128]{2,1,0:T(8,128)(2,1)S(1)} %norm.2.refs_1_), channel_id=1, source_target_pairs={{0,6},{1,3},{2,4},{3,1},{4,2},{5,7},{6,0},{7,5},{8,14},{9,11},{10,... | collective-permute-start | bytes 282632 | tf_op jit(solution)/shard_map/ppermute | solution.py:176
  14.6 0.5 %collective-permute-start.3 = (bf16[2,184,128]{2,1,0:T(8,128)(2,1)S(1)}, bf16[2,184,128]{2,1,0:T(8,128)(2,1)S(1)}, u32[]{:S(2)}, u32[]{:S(2)}) collective-permute-start(bf16[2,184,128]{2,1,0:T(8,128)(2,1)S(1)} %norm.2.refs_1_), channel_id=1, source_target_pairs={{0,4},{1,5},{2,6},{3,7},{4,0},{5,1},{6,2},{7,3},{8,12},{9,13},{10,... | collective-permute-start | bytes 282632 | tf_op jit(solution)/shard_map/ppermute | solution.py:176
  15.1 0.0 collective-permute-done.10.refs_3_
  15.1 0.6 %collective-permute-start.5 = (bf16[2,184,128]{2,1,0:T(8,128)(2,1)S(1)}, bf16[2,184,128]{2,1,0:T(8,128)(2,1)S(1)}, u32[]{:S(2)}, u32[]{:S(2)}) collective-permute-start(bf16[2,184,128]{2,1,0:T(8,128)(2,1)S(1)} %norm.2.refs_1_), channel_id=1, source_target_pairs={{0,2},{1,7},{2,0},{3,5},{4,6},{5,3},{6,4},{7,1},{8,10},{9,15},{10,... | collective-permute-start | bytes 282632 | tf_op jit(solution)/shard_map/ppermute | solution.py:176
  15.7 0.0 collective-permute-done.11.refs_4_
  15.8 0.6 %collective-permute-start.12 = (bf16[6,184,128]{2,1,0:T(8,128)(2,1)S(1)}, bf16[6,184,128]{2,1,0:T(8,128)(2,1)S(1)}, u32[]{:S(2)}, u32[]{:S(2)}) collective-permute-start(bf16[6,184,128]{2,1,0:T(8,128)(2,1)S(1)} %pad_maximum_fusion), channel_id=1, source_target_pairs={{0,1},{1,0},{2,3},{3,2},{4,5},{5,4},{6,7},{7,6},{8,9},{9,8},{10,11... | collective-permute-start | bytes 847880 | tf_op jit(solution)/shard_map/ppermute | solution.py:176
  16.3 2.2 %collective-permute-done.2.refs_0_ = bf16[2,184,128]{2,1,0:T(8,128)(2,1)S(1)} collective-permute-done((bf16[2,184,128]{2,1,0:T(8,128)(2,1)S(1)}, bf16[2,184,128]{2,1,0:T(8,128)(2,1)S(1)}, u32[]{:S(2)}, u32[]{:S(2)}) %collective-permute-start.2) | collective-permute-done | bytes 94240 | tf_op jit(solution)/shard_map/ppermute | solution.py:176
  18.5 0.6 %collective-permute-done.3.refs_1_ = bf16[2,184,128]{2,1,0:T(8,128)(2,1)S(1)} collective-permute-done((bf16[2,184,128]{2,1,0:T(8,128)(2,1)S(1)}, bf16[2,184,128]{2,1,0:T(8,128)(2,1)S(1)}, u32[]{:S(2)}, u32[]{:S(2)}) %collective-permute-start.3) | collective-permute-done | bytes 94240 | tf_op jit(solution)/shard_map/ppermute | solution.py:176
  19.2 0.0 copy-start.1
  19.2 0.0 copy-start.2
  19.2 0.1 collective-permute-start.4
  19.3 0.5 %collective-permute-done.5.refs_2_ = bf16[2,184,128]{2,1,0:T(8,128)(2,1)S(1)} collective-permute-done((bf16[2,184,128]{2,1,0:T(8,128)(2,1)S(1)}, bf16[2,184,128]{2,1,0:T(8,128)(2,1)S(1)}, u32[]{:S(2)}, u32[]{:S(2)}) %collective-permute-start.5) | collective-permute-done | bytes 94240 | tf_op jit(solution)/shard_map/ppermute | solution.py:176
  19.8 0.0 collective-permute-start.6
  19.8 0.0 copy-start.5
  19.8 0.1 copy-done.1
  19.9 0.6 %copy-done.4 = f32[4,12]{1,0:T(4,128)S(1)} copy-done((f32[4,12]{1,0:T(4,128)S(1)}, f32[4,12]{1,0:T(4,128)}, u32[]{:S(2)}) %copy-start.4) | copy-done | bytes 216
  20.5 0.4 %prep.1 = (f32[128,128]{1,0:T(8,128)S(1)}, bf16[128,128]{1,0:T(8,128)(2,1)S(1)}, f32[1,128]{1,0:T(1,128)S(1)}, f32[32,128]{1,0:T(8,128)S(1)}, f32[32,128]{1,0:T(8,128)S(1)}, /*index=5*/f32[2,128]{1,0:T(2,128)S(1)}) custom-call(s32[32,32]{1,0:T(8,128)S(1)} %order.1.order_ref, s32[16,12]{1,0:T(8,128)S(1)} %copy-done.2, s32[1,32]{1,0:T(1,128)S(1)} %bitcast.6, ...), custom_call_target="tpu_custom_call" | custom-call | tf_op jit(solution)/shard_map/prep/pallas_call | solution.py:322
  20.9 0.7 %shard_map.77 = (f32[2,128,128]{2,1,0:T(8,128)S(1)}, f32[2,128]{1,0:T(2,128)S(1)}) custom-call(bf16[2,184,128]{2,1,0:T(8,128)(2,1)S(1)} %norm.3.refs_0_, bf16[2,184,128]{2,1,0:T(8,128)(2,1)S(1)} %norm.2.refs_1_, bf16[2,184,128]{2,1,0:T(8,128)(2,1)S(1)} %collective-permute-done.9.refs_2_, bf16[2,184,128]{2,1,0:T(8,128)(2,1)S(1)} %collective-permute-done.10.refs_3_, ...), custom_call_target="tpu_custom_call" | custom-call | tf_op jit(solution)/shard_map/pallas_call | solution.py:346
  21.6 0.7 %shard_map.78 = (f32[2,128,128]{2,1,0:T(8,128)S(1)}, f32[2,128]{1,0:T(2,128)S(1)}) custom-call(bf16[4,184,128]{2,1,0:T(8,128)(2,1)S(1)} %collective-permute-done.8.refs_0_, bf16[6,184,128]{2,1,0:T(8,128)(2,1)S(1)} %collective-permute-done.12.refs_1_, bf16[128,128]{1,0:T(8,128)(2,1)S(1)} %get-tuple-element.16.refs_5_.refs_2_.refs_3_, ...), custom_call_target="tpu_custom_call" | custom-call | tf_op jit(solution)/shard_map/pallas_call | solution.py:346
  22.4 0.5 %shard_map.79 = (f32[2,128,128]{2,1,0:T(8,128)S(1)}, f32[2,128]{1,0:T(2,128)S(1)}) custom-call(bf16[2,184,128]{2,1,0:T(8,128)(2,1)S(1)} %collective-permute-done.2.refs_0_, bf16[2,184,128]{2,1,0:T(8,128)(2,1)S(1)} %collective-permute-done.3.refs_1_, bf16[2,184,128]{2,1,0:T(8,128)(2,1)S(1)} %collective-permute-done.5.refs_2_, ...), custom_call_target="tpu_custom_call" | custom-call | tf_op jit(solution)/shard_map/pallas_call | solution.py:346
  22.9 1.3 %shard_map.80 = (f32[128,128]{1,0:T(8,128)}, f32[1,4]{1,0:T(1,128)}) custom-call(bf16[4,184,128]{2,1,0:T(8,128)(2,1)S(1)} %collective-permute-done.4.refs_0_, bf16[2,184,128]{2,1,0:T(8,128)(2,1)S(1)} %collective-permute-done.6.refs_1_, bf16[128,128]{1,0:T(8,128)(2,1)S(1)} %get-tuple-element.16.refs_5_.refs_2_.refs_3_, ...), custom_call_target="tpu_custom_call" | custom-call | tf_op jit(solution)/shard_map/pallas_call | solution.py:346
  (17 shorter events, 0.1 us)
Async XLA Ops:
  0.6 5.7 %copy-start.3 = (s32[8]{0:T(128)S(1)}, s32[8]{0:T(128)}, u32[]{:S(2)}) copy-start(s32[8]{0:T(128)} %param.8) | copy-start | bytes 100
  0.6 5.7 %collective-permute-start.7 = (bf16[1,184,128]{2,1,0:T(8,128)(2,1)}, bf16[1,184,128]{2,1,0:T(8,128)(2,1)S(1)}, u32[]{:S(2)}, u32[]{:S(2)}) collective-permute-start(bf16[1,184,128]{2,1,0:T(8,128)(2,1)} %refs_0_.1), channel_id=1, source_target_pairs={{0,8},{1,9},{2,10},{3,11},{4,12},{5,13},{6,14},{7,15},{8,0},{9,1},... | collective-permute-start | bytes 141320 | tf_op jit(solution)/shard_map/ppermute | solution.py:176
  3.8 7.1 %collective-permute-start = (bf16[1,184,128]{2,1,0:T(8,128)(2,1)}, bf16[1,184,128]{2,1,0:T(8,128)(2,1)S(1)}, u32[]{:S(2)}, u32[]{:S(2)}) collective-permute-start(bf16[1,184,128]{2,1,0:T(8,128)(2,1)} %refs_0_.1), channel_id=1, source_target_pairs={{0,24},{1,25},{2,26},{3,27},{4,28},{5,29},{6,30},{7,31},{8,16},{9,... | collective-permute-start | bytes 141320 | tf_op jit(solution)/shard_map/ppermute | solution.py:176
  6.2 5.7 %collective-permute-start.1 = (bf16[1,184,128]{2,1,0:T(8,128)(2,1)}, bf16[1,184,128]{2,1,0:T(8,128)(2,1)S(1)}, u32[]{:S(2)}, u32[]{:S(2)}) collective-permute-start(bf16[1,184,128]{2,1,0:T(8,128)(2,1)} %refs_0_.1), channel_id=1, source_target_pairs={{0,16},{1,17},{2,18},{3,19},{4,20},{5,21},{6,22},{7,23},{8,24},{9,... | collective-permute-start | bytes 141320 | tf_op jit(solution)/shard_map/ppermute | solution.py:176
  6.4 0.8 %copy-start = (bf16[1,184,128]{2,1,0:T(8,128)(2,1)S(1)}, bf16[1,184,128]{2,1,0:T(8,128)(2,1)}, u32[]{:S(2)}) copy-start(bf16[1,184,128]{2,1,0:T(8,128)(2,1)} %refs_0_.1) | copy-start | bytes 141316
  7.3 7.8 %collective-permute-start.10 = (bf16[2,184,128]{2,1,0:T(8,128)(2,1)S(1)}, bf16[2,184,128]{2,1,0:T(8,128)(2,1)S(1)}, u32[]{:S(2)}, u32[]{:S(2)}) collective-permute-start(bf16[2,184,128]{2,1,0:T(8,128)(2,1)S(1)} %norm.3.refs_0_), channel_id=1, source_target_pairs={{0,2},{1,3},{2,0},{3,1},{4,6},{5,7},{6,4},{7,5},{8,10},{9,11},{10,... | collective-permute-start | bytes 282632 | tf_op jit(solution)/shard_map/ppermute | solution.py:176
  9.0 6.7 %collective-permute-start.11 = (bf16[2,184,128]{2,1,0:T(8,128)(2,1)S(1)}, bf16[2,184,128]{2,1,0:T(8,128)(2,1)S(1)}, u32[]{:S(2)}, u32[]{:S(2)}) collective-permute-start(bf16[2,184,128]{2,1,0:T(8,128)(2,1)S(1)} %norm.3.refs_0_), channel_id=1, source_target_pairs={{0,6},{1,7},{2,4},{3,5},{4,2},{5,3},{6,0},{7,1},{8,14},{9,15},{10,... | collective-permute-start | bytes 282632 | tf_op jit(solution)/shard_map/ppermute | solution.py:176
  10.4 5.3 %collective-permute-start.9 = (bf16[2,184,128]{2,1,0:T(8,128)(2,1)S(1)}, bf16[2,184,128]{2,1,0:T(8,128)(2,1)S(1)}, u32[]{:S(2)}, u32[]{:S(2)}) collective-permute-start(bf16[2,184,128]{2,1,0:T(8,128)(2,1)S(1)} %norm.3.refs_0_), channel_id=1, source_target_pairs={{0,4},{1,5},{2,6},{3,7},{4,0},{5,1},{6,2},{7,3},{8,12},{9,13},{10,... | collective-permute-start | bytes 282632 | tf_op jit(solution)/shard_map/ppermute | solution.py:176
  12.1 6.4 %collective-permute-start.2 = (bf16[2,184,128]{2,1,0:T(8,128)(2,1)S(1)}, bf16[2,184,128]{2,1,0:T(8,128)(2,1)S(1)}, u32[]{:S(2)}, u32[]{:S(2)}) collective-permute-start(bf16[2,184,128]{2,1,0:T(8,128)(2,1)S(1)} %norm.2.refs_1_), channel_id=1, source_target_pairs={{0,6},{1,3},{2,4},{3,1},{4,2},{5,7},{6,0},{7,5},{8,14},{9,11},{10,... | collective-permute-start | bytes 282632 | tf_op jit(solution)/shard_map/ppermute | solution.py:176
  14.6 4.6 %collective-permute-start.3 = (bf16[2,184,128]{2,1,0:T(8,128)(2,1)S(1)}, bf16[2,184,128]{2,1,0:T(8,128)(2,1)S(1)}, u32[]{:S(2)}, u32[]{:S(2)}) collective-permute-start(bf16[2,184,128]{2,1,0:T(8,128)(2,1)S(1)} %norm.2.refs_1_), channel_id=1, source_target_pairs={{0,4},{1,5},{2,6},{3,7},{4,0},{5,1},{6,2},{7,3},{8,12},{9,13},{10,... | collective-permute-start | bytes 282632 | tf_op jit(solution)/shard_map/ppermute | solution.py:176
  15.1 4.7 %collective-permute-start.5 = (bf16[2,184,128]{2,1,0:T(8,128)(2,1)S(1)}, bf16[2,184,128]{2,1,0:T(8,128)(2,1)S(1)}, u32[]{:S(2)}, u32[]{:S(2)}) collective-permute-start(bf16[2,184,128]{2,1,0:T(8,128)(2,1)S(1)} %norm.2.refs_1_), channel_id=1, source_target_pairs={{0,2},{1,7},{2,0},{3,5},{4,6},{5,3},{6,4},{7,1},{8,10},{9,15},{10,... | collective-permute-start | bytes 282632 | tf_op jit(solution)/shard_map/ppermute | solution.py:176
  15.7 5.9 %collective-permute-start.8 = (bf16[4,184,128]{2,1,0:T(8,128)(2,1)S(1)}, bf16[4,184,128]{2,1,0:T(8,128)(2,1)S(1)}, u32[]{:S(2)}, u32[]{:S(2)}) collective-permute-start(bf16[4,184,128]{2,1,0:T(8,128)(2,1)S(1)} %pad_maximum_fusion.2), channel_id=1, source_target_pairs={{0,1},{1,0},{2,3},{3,2},{4,5},{5,4},{6,7},{7,6},{8,9},{9,8},{10,11... | collective-permute-start | bytes 565256 | tf_op jit(solution)/shard_map/ppermute | solution.py:176
  15.8 5.9 %collective-permute-start.12 = (bf16[6,184,128]{2,1,0:T(8,128)(2,1)S(1)}, bf16[6,184,128]{2,1,0:T(8,128)(2,1)S(1)}, u32[]{:S(2)}, u32[]{:S(2)}) collective-permute-start(bf16[6,184,128]{2,1,0:T(8,128)(2,1)S(1)} %pad_maximum_fusion), channel_id=1, source_target_pairs={{0,1},{1,0},{2,3},{3,2},{4,5},{5,4},{6,7},{7,6},{8,9},{9,8},{10,11... | collective-permute-start | bytes 847880 | tf_op jit(solution)/shard_map/ppermute | solution.py:176
  19.2 0.8 %copy-start.1 = (bf16[4,32,128]{2,1,0:T(8,128)(2,1)S(1)}, bf16[4,32,128]{2,1,0:T(8,128)(2,1)}, u32[]{:S(2)}) copy-start(bf16[4,32,128]{2,1,0:T(8,128)(2,1)} %query_ref.1) | copy-start | bytes 98308
  19.2 0.8 %copy-start.2 = (s32[16,12]{1,0:T(8,128)S(1)}, s32[16,12]{1,0:T(8,128)}, u32[]{:S(2)}) copy-start(s32[16,12]{1,0:T(8,128)} %cand_ref.1) | copy-start | bytes 2308
  19.2 3.8 %collective-permute-start.4 = (bf16[4,184,128]{2,1,0:T(8,128)(2,1)S(1)}, bf16[4,184,128]{2,1,0:T(8,128)(2,1)S(1)}, u32[]{:S(2)}, u32[]{:S(2)}) collective-permute-start(bf16[4,184,128]{2,1,0:T(8,128)(2,1)S(1)} %pad_maximum_fusion.1), channel_id=1, source_target_pairs={{0,1},{1,0},{2,3},{3,2},{4,5},{5,4},{6,7},{7,6},{8,9},{9,8},{10,11... | collective-permute-start | bytes 565256 | tf_op jit(solution)/shard_map/ppermute | solution.py:176
  19.8 3.1 %collective-permute-start.6 = (bf16[2,184,128]{2,1,0:T(8,128)(2,1)S(1)}, bf16[2,184,128]{2,1,0:T(8,128)(2,1)S(1)}, u32[]{:S(2)}, u32[]{:S(2)}) collective-permute-start(bf16[2,184,128]{2,1,0:T(8,128)(2,1)S(1)} %collective-permute-done.5.refs_2_), channel_id=1, source_target_pairs={{0,1},{1,0},{2,3},{3,2},{4,5},{5,4},{6,7},{7,6},{8,9},{9,8},{10,11... | collective-permute-start | bytes 282632 | tf_op jit(solution)/shard_map/ppermute | solution.py:176
  19.8 0.7 %copy-start.4 = (f32[4,12]{1,0:T(4,128)S(1)}, f32[4,12]{1,0:T(4,128)}, u32[]{:S(2)}) copy-start(f32[4,12]{1,0:T(4,128)} %teacher_ref.1) | copy-start | bytes 580
  19.8 0.7 %copy-start.5 = (s32[32]{0:T(128)S(1)}, s32[32]{0:T(128)}, u32[]{:S(2)}) copy-start(s32[32]{0:T(128)} %param.10) | copy-start | bytes 388
